TPU v7x, 32 devices: a whole 2x2x4 slice. The times are simulated.
32 devices in a mesh: band: 8 (over z, x), lon: 4 (over y, core).
Axes of the slice: x: 2, y: 2, z: 4, core: 2. Of those that a mesh axis runs over, the one named last changes fastest.
Arguments:
- coefficients: bfloat16 [8, 640, 4, 64], P('lon', 'band'), may hold values from -6 to 6
- cycle_length: int32 [64], replicated, may hold values from 20 to 5136, as said below
- row_latitude: int32 [64], replicated, may hold values from 0 to 63, each once
- pair_band: int32 [640], replicated, may hold values from 0 to 7, as said below
- gridpoint_factor: bfloat16 [64, 5632], P('band', 'lon'), may hold values from 0.5 to 2
Outputs:
- grid_values: bfloat16 [8, 64, 5632], P(None, 'band', 'lon')
- tendencies: bfloat16 [8, 640, 4, 64], P('lon', 'band')
Inputs may be any that keep to these rules, and one draw needn't show every extreme that they name: `cycle_length`: each entry is 20 + 4 i for a whole number i; some entry equals 5136. `pair_band`: each band owns at most 80 pairs and some band owns exactly that many. `row_latitude`: each latitude appears once.
All inputs are finite; a program needn't handle non-finite values.
Results may differ from a plain program's by a relative error of at most 0.0068.
Values may be sent and summed in bfloat16 or wider, within the bound.
A program may use at most 128 MiB of HBM per device.

v0:
```python
import math

import jax
import jax.numpy as jnp
from jax import lax
from jax.sharding import PartitionSpec as P

TWO_PI = 2.0 * math.pi


def slot_maps(pair_band, band_count, slot_count, wave_count):
    pair_count = pair_band.shape[0]
    onehot = (pair_band[:, None] == jnp.arange(band_count, dtype=jnp.int32)[None, :]).astype(
        jnp.int32
    )
    before = jnp.cumsum(onehot, axis=0) - onehot
    position_within_band = jnp.sum(before * onehot, axis=1)
    slot_of_pair = pair_band * slot_count + position_within_band
    slot_of_wave = jnp.concatenate([slot_of_pair, slot_of_pair[::-1]])
    member_of_wave = (jnp.arange(wave_count, dtype=jnp.int32) >= pair_count).astype(jnp.int32)
    pair_of_slot = (
        jnp.full((band_count * slot_count,), -1, jnp.int32)
        .at[slot_of_pair]
        .set(jnp.arange(pair_count, dtype=jnp.int32))
    )
    occupied = pair_of_slot >= 0
    first_wave = jnp.where(occupied, pair_of_slot, 0)
    wave_of_slot = jnp.stack([first_wave, wave_count - 1 - first_wave], axis=1)
    return (slot_of_wave, member_of_wave, wave_of_slot, occupied)


def cycle_table(lengths, wave_count, points):
    places = jnp.arange(points, dtype=jnp.int32)
    low_index = jnp.arange(32, dtype=jnp.int32)
    high_index = 32 * jnp.arange(wave_count // 32, dtype=jnp.int32)

    def single_period(length):
        scale = TWO_PI / length.astype(jnp.float32)
        fine = (low_index[:, None] * places[None, :] % length).astype(jnp.float32) * scale
        coarse = (high_index[:, None] * places[None, :] % length).astype(jnp.float32) * scale
        cos_fine, sin_fine = (jnp.cos(fine), jnp.sin(fine))
        cos_coarse, sin_coarse = (jnp.cos(coarse), jnp.sin(coarse))
        cosine = cos_coarse[:, None, :] * cos_fine[None] - sin_coarse[:, None, :] * sin_fine[None]
        sine = sin_coarse[:, None, :] * cos_fine[None] + cos_coarse[:, None, :] * sin_fine[None]
        return jnp.stack(
            [cosine.reshape(wave_count, points), -sine.reshape(wave_count, points)]
        ).astype(jnp.bfloat16)

    return lax.map(single_period, lengths)


def turn_factors(lengths, wave_count, offsets):
    wave_index = jnp.arange(wave_count, dtype=jnp.int32)
    turn_count = offsets[:, None, None] * wave_index[None, None, :] % lengths[None, :, None]
    angles = turn_count.astype(jnp.float32) * (TWO_PI / lengths.astype(jnp.float32))[None, :, None]
    return (jnp.cos(angles), jnp.sin(angles))


def kept_mask(lengths, wave_count):
    wave_index = jnp.arange(wave_count, dtype=jnp.int32)
    return (2 * wave_index[None, :] < lengths[:, None]).astype(jnp.float32)


def weighted(fourier, lengths):
    wave_count = fourier.shape[3]
    wave_index = jnp.arange(wave_count, dtype=jnp.int32)
    doubled = jnp.where(wave_index == 0, 1.0, 2.0).astype(jnp.float32)
    factor = (
        doubled[None, :]
        * kept_mask(lengths, wave_count)
        * lax.rsqrt(lengths.astype(jnp.float32))[:, None]
    )
    return fourier.astype(jnp.float32) * factor[None, :, None, :]


def turned(scaled, cosines, sine_values):
    real_part = scaled[:, None, :, 0, :]
    imag_part = scaled[:, None, :, 1, :]
    new_real = real_part * cosines[None] - imag_part * sine_values[None]
    new_imag = real_part * sine_values[None] + imag_part * cosines[None]
    return jnp.stack([new_real, new_imag], axis=3).astype(jnp.bfloat16)


def synthesize(coeffs, tables, lengths, offsets):
    values = jnp.einsum("fdrtm,rtml->frdl", coeffs, tables, preferred_element_type=jnp.float32)
    places = offsets[None, :, None] + jnp.arange(tables.shape[3], dtype=jnp.int32)[None, None, :]
    inside = places < lengths[:, None, None]
    return jnp.where(inside[None], values, 0.0).astype(jnp.bfloat16)


def analyze(values, tables):
    return jnp.einsum("frdl,rtml->fdrtm", values, tables, preferred_element_type=jnp.float32)


def untwist(partials, cosines, sine_values):
    real_part = partials[:, :, :, 0, :]
    imag_part = partials[:, :, :, 1, :]
    new_real = jnp.sum(real_part * cosines[None] + imag_part * sine_values[None], axis=1)
    new_imag = jnp.sum(imag_part * cosines[None] - real_part * sine_values[None], axis=1)
    return jnp.stack([new_real, new_imag], axis=2)


def finish(summed, lengths):
    wave_count = summed.shape[3]
    factor = kept_mask(lengths, wave_count) * lax.rsqrt(lengths.astype(jnp.float32))[:, None]
    return (summed * factor[None, :, None, :]).astype(jnp.bfloat16)


def on_device(coefficients, cycle_length, row_latitude, pair_band, gridpoint_factor):
    band_count = lax.axis_size("band")
    lane_count = lax.axis_size("lon")
    band_index = lax.axis_index("band")
    slot_count = coefficients.shape[1]
    wave_count = 2 * pair_band.shape[0]
    row_count = gridpoint_factor.shape[0]
    points = gridpoint_factor.shape[1]
    slot_of_wave, member_of_wave, wave_of_slot, occupied = slot_maps(
        pair_band, band_count, slot_count, wave_count
    )
    band_lats = lax.dynamic_slice_in_dim(row_latitude, band_index * row_count, row_count)
    lengths = jnp.take(cycle_length, band_lats)
    tables = cycle_table(lengths, wave_count, points)
    by_row = jnp.take(coefficients, row_latitude, axis=3)
    arrived = lax.all_to_all(by_row, "band", split_axis=3, concat_axis=1, tiled=True)
    split_view = arrived.reshape(arrived.shape[0], band_count * slot_count, 2, 2, row_count)
    picked = split_view[:, slot_of_wave, member_of_wave]
    fourier = jnp.transpose(picked, (0, 3, 2, 1))
    whole_factor = lax.all_gather(gridpoint_factor, "lon", axis=1, tiled=True)
    offsets = points * jnp.arange(lane_count, dtype=jnp.int32)
    cosines, sine_values = turn_factors(lengths, wave_count, offsets)
    coeffs = turned(weighted(fourier, lengths), cosines, sine_values)
    blocks = synthesize(coeffs, tables, lengths, offsets)
    cycle_blocks = blocks.reshape(blocks.shape[0], row_count, lane_count * points)
    grid_rows = lax.all_to_all(cycle_blocks, "lon", split_axis=2, concat_axis=0, tiled=True)
    products = (whole_factor.astype(jnp.float32)[None] * cycle_blocks.astype(jnp.float32)).astype(
        jnp.bfloat16
    )
    partials = analyze(products.reshape(products.shape[0], row_count, lane_count, points), tables)
    summed = untwist(partials, cosines, sine_values)
    finished = finish(summed, lengths)
    reordered = jnp.transpose(finished, (0, 3, 2, 1))
    placed = reordered[:, wave_of_slot]
    placed = jnp.where(occupied[None, :, None, None, None], placed, jnp.zeros_like(placed))
    packed = placed.reshape(placed.shape[0], band_count * slot_count, 4, row_count)
    returned = lax.all_to_all(packed, "band", split_axis=1, concat_axis=3, tiled=True)
    total_rows = row_latitude.shape[0]
    inverse_rows = (
        jnp.zeros((total_rows,), jnp.int32)
        .at[row_latitude]
        .set(jnp.arange(total_rows, dtype=jnp.int32))
    )
    tendencies = jnp.take(returned, inverse_rows, axis=3)
    return (grid_rows, tendencies)


def solution(mesh):
    return jax.shard_map(
        on_device,
        mesh=mesh,
        in_specs=(P("lon", "band", None, None), P(), P(), P(), P("band", "lon")),
        out_specs=(P(None, "band", "lon"), P("lon", "band", None, None)),
        check_vma=False,
    )
```

profile of v0, /device:TPU:0, one launch (start us, length us, event | category | flops | bytes accessed | tf_op | source)
XLA Modules:
  0.0 245.2 jit_solution(14467738024473252951)
XLA Ops:
  2.0 0.8 scatter_custom_fusion.1
  2.8 1.0 gather_fusion.3
  3.9 0.8 copy.60
  4.7 7.3 %all-to-all-start = ((bf16[2,80,4,64]{1,2,0,3:T(4,128)(2,1)}), bf16[2,80,4,64]{1,2,0,3:T(4,128)(2,1)S(1)}, u32[]{:S(2)}, u32[]{:S(2)}) async-start(bf16[2,80,4,64]{1,2,0,3:T(4,128)(2,1)} %copy.60), calls=%async_computation | async-start | bytes 262144 | tf_op jit(solution)/shard_map/all_to_all | solution.py:124
  12.0 0.7 compare_select_fusion.9
  12.7 1.3 gather_fusion
  14.0 0.7 convert_rsqrt_fusion
  15.5 1.4 reduce-window.6
  17.4 0.8 fusion.55
  19.1 4.3 %scatter_custom_fusion = s32[640]{0:T(1024)S(1)} fusion(s32[640]{0:T(1024)S(1)} %get-tuple-element.81, s32[640]{0:T(1024)S(1)} %iota.73, s32[]{:T(128)} %constant.72.clone.1), kind=kCustom, calls=%fused_computation.115 | custom fusion | bytes 2564 | tf_op jit(solution)/shard_map/scatter | solution.py:24
  23.4 115.3 %while.12 = (s32[]{:T(128)}, bf16[8,2,1280,1408]{3,2,1,0:T(8,128)(2,1)}, s32[8]{0:T(128)S(1)}, s32[]{:T(128)}, f32[]{:T(128)}, /*index=5*/s32[]{:T(128)}) while((s32[]{:T(128)}, bf16[8,2,1280,1408]{3,2,1,0:T(8,128)(2,1)}, s32[8]{0:T(128)S(1)}, s32[]{:T(128)}, f32[]{:T(128)}, /*index=5*/s32[]{:T(128)}) %tuple.51), condition=%wide.region_1.2_spmd.clone.clone, body=%wide.region_0.0_spmd.clone.clone.sunk | while | flops 31651888 | bytes 23249376 | solution.py:49
  26.2 2.4 fusion.72
  28.6 3.1 %fusion.73 = (f32[40,1408]{1,0:T(8,128)S(1)}, f32[40,1408]{1,0:T(8,128)S(1)}) fusion(f32[]{:T(128)S(6)} %div.13, s32[]{:T(128)S(6)} %select_n.238, s32[40]{0:T(128)S(1)} %iota_multiply_fusion.7, pred[]{:T(512)S(6)} %lt.262), kind=kLoop, calls=%fused_computation.22.clone.1 | loop fusion | flops 563200 | bytes 450729 | tf_op jit(solution)/shard_map/while/body/eval_jaxpr/cos | solution.py:42
  31.7 2.7 %subtract_convert_fusion.3 = (bf16[40,32,1408]{2,1,0:T(8,128)(2,1)S(1)}, bf16[40,32,1408]{2,1,0:T(8,128)(2,1)S(1)}) fusion(f32[32,1408]{1,0:T(8,128)S(1)} %get-tuple-element.128, f32[40,1408]{1,0:T(8,128)S(1)} %get-tuple-element.129, f32[32,1408]{1,0:T(8,128)S(1)} %get-tuple-element.130, f32[40,1408]{1,0:T(8,128)S(1)} %get-tuple-element.131), kind=kLoop, calls=%fused_computation.12.clone.1 | loop fusion | flops 16220160 | bytes 8019968 | tf_op jit(solution)/shard_map/convert.3
  34.4 3.5 %maximum_dynamic-update-slice_fusion.2 = bf16[8,2,1280,1408]{3,2,1,0:T(8,128)(2,1)} fusion(bf16[8,2,1280,1408]{3,2,1,0:T(8,128)(2,1)} %get-tuple-element.141, s32[]{:T(128)S(6)} %copy.97, bf16[1,1,1280,1408]{3,2,1,0:T(8,128)(2,1)S(1)} %bitcast.106, bf16[1,1,1280,1408]{3,2,1,0:T(8,128)(2,1)S(1)} %bitcast.105), kind=kLoop, calls=%fused_computation.10.clone.1 | loop fusion | flops 14417920 | bytes 14417924 | tf_op jit(solution)/shard_map/while/body/jit(dynamic_update_index_in_dim)/dynamic_update_slice | solution.py:49
  40.6 2.4 fusion.72
  43.1 3.1 %fusion.73 = (f32[40,1408]{1,0:T(8,128)S(1)}, f32[40,1408]{1,0:T(8,128)S(1)}) fusion(f32[]{:T(128)S(6)} %div.13, s32[]{:T(128)S(6)} %select_n.238, s32[40]{0:T(128)S(1)} %iota_multiply_fusion.7, pred[]{:T(512)S(6)} %lt.262), kind=kLoop, calls=%fused_computation.22.clone.1 | loop fusion | flops 563200 | bytes 450729 | tf_op jit(solution)/shard_map/while/body/eval_jaxpr/cos | solution.py:42
  46.1 2.7 %subtract_convert_fusion.3 = (bf16[40,32,1408]{2,1,0:T(8,128)(2,1)S(1)}, bf16[40,32,1408]{2,1,0:T(8,128)(2,1)S(1)}) fusion(f32[32,1408]{1,0:T(8,128)S(1)} %get-tuple-element.128, f32[40,1408]{1,0:T(8,128)S(1)} %get-tuple-element.129, f32[32,1408]{1,0:T(8,128)S(1)} %get-tuple-element.130, f32[40,1408]{1,0:T(8,128)S(1)} %get-tuple-element.131), kind=kLoop, calls=%fused_computation.12.clone.1 | loop fusion | flops 16220160 | bytes 8019968 | tf_op jit(solution)/shard_map/convert.3
  48.8 3.5 %maximum_dynamic-update-slice_fusion.2 = bf16[8,2,1280,1408]{3,2,1,0:T(8,128)(2,1)} fusion(bf16[8,2,1280,1408]{3,2,1,0:T(8,128)(2,1)} %get-tuple-element.141, s32[]{:T(128)S(6)} %copy.97, bf16[1,1,1280,1408]{3,2,1,0:T(8,128)(2,1)S(1)} %bitcast.106, bf16[1,1,1280,1408]{3,2,1,0:T(8,128)(2,1)S(1)} %bitcast.105), kind=kLoop, calls=%fused_computation.10.clone.1 | loop fusion | flops 14417920 | bytes 14417924 | tf_op jit(solution)/shard_map/while/body/jit(dynamic_update_index_in_dim)/dynamic_update_slice | solution.py:49
  55.1 2.4 fusion.72
  57.5 3.1 %fusion.73 = (f32[40,1408]{1,0:T(8,128)S(1)}, f32[40,1408]{1,0:T(8,128)S(1)}) fusion(f32[]{:T(128)S(6)} %div.13, s32[]{:T(128)S(6)} %select_n.238, s32[40]{0:T(128)S(1)} %iota_multiply_fusion.7, pred[]{:T(512)S(6)} %lt.262), kind=kLoop, calls=%fused_computation.22.clone.1 | loop fusion | flops 563200 | bytes 450729 | tf_op jit(solution)/shard_map/while/body/eval_jaxpr/cos | solution.py:42
  60.6 2.7 %subtract_convert_fusion.3 = (bf16[40,32,1408]{2,1,0:T(8,128)(2,1)S(1)}, bf16[40,32,1408]{2,1,0:T(8,128)(2,1)S(1)}) fusion(f32[32,1408]{1,0:T(8,128)S(1)} %get-tuple-element.128, f32[40,1408]{1,0:T(8,128)S(1)} %get-tuple-element.129, f32[32,1408]{1,0:T(8,128)S(1)} %get-tuple-element.130, f32[40,1408]{1,0:T(8,128)S(1)} %get-tuple-element.131), kind=kLoop, calls=%fused_computation.12.clone.1 | loop fusion | flops 16220160 | bytes 8019968 | tf_op jit(solution)/shard_map/convert.3
  63.3 3.4 %maximum_dynamic-update-slice_fusion.2 = bf16[8,2,1280,1408]{3,2,1,0:T(8,128)(2,1)} fusion(bf16[8,2,1280,1408]{3,2,1,0:T(8,128)(2,1)} %get-tuple-element.141, s32[]{:T(128)S(6)} %copy.97, bf16[1,1,1280,1408]{3,2,1,0:T(8,128)(2,1)S(1)} %bitcast.106, bf16[1,1,1280,1408]{3,2,1,0:T(8,128)(2,1)S(1)} %bitcast.105), kind=kLoop, calls=%fused_computation.10.clone.1 | loop fusion | flops 14417920 | bytes 14417924 | tf_op jit(solution)/shard_map/while/body/jit(dynamic_update_index_in_dim)/dynamic_update_slice | solution.py:49
  69.5 2.4 fusion.72
  71.9 3.1 %fusion.73 = (f32[40,1408]{1,0:T(8,128)S(1)}, f32[40,1408]{1,0:T(8,128)S(1)}) fusion(f32[]{:T(128)S(6)} %div.13, s32[]{:T(128)S(6)} %select_n.238, s32[40]{0:T(128)S(1)} %iota_multiply_fusion.7, pred[]{:T(512)S(6)} %lt.262), kind=kLoop, calls=%fused_computation.22.clone.1 | loop fusion | flops 563200 | bytes 450729 | tf_op jit(solution)/shard_map/while/body/eval_jaxpr/cos | solution.py:42
  75.0 2.7 %subtract_convert_fusion.3 = (bf16[40,32,1408]{2,1,0:T(8,128)(2,1)S(1)}, bf16[40,32,1408]{2,1,0:T(8,128)(2,1)S(1)}) fusion(f32[32,1408]{1,0:T(8,128)S(1)} %get-tuple-element.128, f32[40,1408]{1,0:T(8,128)S(1)} %get-tuple-element.129, f32[32,1408]{1,0:T(8,128)S(1)} %get-tuple-element.130, f32[40,1408]{1,0:T(8,128)S(1)} %get-tuple-element.131), kind=kLoop, calls=%fused_computation.12.clone.1 | loop fusion | flops 16220160 | bytes 8019968 | tf_op jit(solution)/shard_map/convert.3
  77.7 3.5 %maximum_dynamic-update-slice_fusion.2 = bf16[8,2,1280,1408]{3,2,1,0:T(8,128)(2,1)} fusion(bf16[8,2,1280,1408]{3,2,1,0:T(8,128)(2,1)} %get-tuple-element.141, s32[]{:T(128)S(6)} %copy.97, bf16[1,1,1280,1408]{3,2,1,0:T(8,128)(2,1)S(1)} %bitcast.106, bf16[1,1,1280,1408]{3,2,1,0:T(8,128)(2,1)S(1)} %bitcast.105), kind=kLoop, calls=%fused_computation.10.clone.1 | loop fusion | flops 14417920 | bytes 14417924 | tf_op jit(solution)/shard_map/while/body/jit(dynamic_update_index_in_dim)/dynamic_update_slice | solution.py:49
  83.9 2.4 fusion.72
  86.3 3.1 %fusion.73 = (f32[40,1408]{1,0:T(8,128)S(1)}, f32[40,1408]{1,0:T(8,128)S(1)}) fusion(f32[]{:T(128)S(6)} %div.13, s32[]{:T(128)S(6)} %select_n.238, s32[40]{0:T(128)S(1)} %iota_multiply_fusion.7, pred[]{:T(512)S(6)} %lt.262), kind=kLoop, calls=%fused_computation.22.clone.1 | loop fusion | flops 563200 | bytes 450729 | tf_op jit(solution)/shard_map/while/body/eval_jaxpr/cos | solution.py:42
  89.4 2.7 %subtract_convert_fusion.3 = (bf16[40,32,1408]{2,1,0:T(8,128)(2,1)S(1)}, bf16[40,32,1408]{2,1,0:T(8,128)(2,1)S(1)}) fusion(f32[32,1408]{1,0:T(8,128)S(1)} %get-tuple-element.128, f32[40,1408]{1,0:T(8,128)S(1)} %get-tuple-element.129, f32[32,1408]{1,0:T(8,128)S(1)} %get-tuple-element.130, f32[40,1408]{1,0:T(8,128)S(1)} %get-tuple-element.131), kind=kLoop, calls=%fused_computation.12.clone.1 | loop fusion | flops 16220160 | bytes 8019968 | tf_op jit(solution)/shard_map/convert.3
  92.1 3.5 %maximum_dynamic-update-slice_fusion.2 = bf16[8,2,1280,1408]{3,2,1,0:T(8,128)(2,1)} fusion(bf16[8,2,1280,1408]{3,2,1,0:T(8,128)(2,1)} %get-tuple-element.141, s32[]{:T(128)S(6)} %copy.97, bf16[1,1,1280,1408]{3,2,1,0:T(8,128)(2,1)S(1)} %bitcast.106, bf16[1,1,1280,1408]{3,2,1,0:T(8,128)(2,1)S(1)} %bitcast.105), kind=kLoop, calls=%fused_computation.10.clone.1 | loop fusion | flops 14417920 | bytes 14417924 | tf_op jit(solution)/shard_map/while/body/jit(dynamic_update_index_in_dim)/dynamic_update_slice | solution.py:49
  98.3 2.4 fusion.72
  100.7 3.1 %fusion.73 = (f32[40,1408]{1,0:T(8,128)S(1)}, f32[40,1408]{1,0:T(8,128)S(1)}) fusion(f32[]{:T(128)S(6)} %div.13, s32[]{:T(128)S(6)} %select_n.238, s32[40]{0:T(128)S(1)} %iota_multiply_fusion.7, pred[]{:T(512)S(6)} %lt.262), kind=kLoop, calls=%fused_computation.22.clone.1 | loop fusion | flops 563200 | bytes 450729 | tf_op jit(solution)/shard_map/while/body/eval_jaxpr/cos | solution.py:42
  103.8 2.7 %subtract_convert_fusion.3 = (bf16[40,32,1408]{2,1,0:T(8,128)(2,1)S(1)}, bf16[40,32,1408]{2,1,0:T(8,128)(2,1)S(1)}) fusion(f32[32,1408]{1,0:T(8,128)S(1)} %get-tuple-element.128, f32[40,1408]{1,0:T(8,128)S(1)} %get-tuple-element.129, f32[32,1408]{1,0:T(8,128)S(1)} %get-tuple-element.130, f32[40,1408]{1,0:T(8,128)S(1)} %get-tuple-element.131), kind=kLoop, calls=%fused_computation.12.clone.1 | loop fusion | flops 16220160 | bytes 8019968 | tf_op jit(solution)/shard_map/convert.3
  106.5 3.5 %maximum_dynamic-update-slice_fusion.2 = bf16[8,2,1280,1408]{3,2,1,0:T(8,128)(2,1)} fusion(bf16[8,2,1280,1408]{3,2,1,0:T(8,128)(2,1)} %get-tuple-element.141, s32[]{:T(128)S(6)} %copy.97, bf16[1,1,1280,1408]{3,2,1,0:T(8,128)(2,1)S(1)} %bitcast.106, bf16[1,1,1280,1408]{3,2,1,0:T(8,128)(2,1)S(1)} %bitcast.105), kind=kLoop, calls=%fused_computation.10.clone.1 | loop fusion | flops 14417920 | bytes 14417924 | tf_op jit(solution)/shard_map/while/body/jit(dynamic_update_index_in_dim)/dynamic_update_slice | solution.py:49
  112.7 2.4 fusion.72
  115.2 3.1 %fusion.73 = (f32[40,1408]{1,0:T(8,128)S(1)}, f32[40,1408]{1,0:T(8,128)S(1)}) fusion(f32[]{:T(128)S(6)} %div.13, s32[]{:T(128)S(6)} %select_n.238, s32[40]{0:T(128)S(1)} %iota_multiply_fusion.7, pred[]{:T(512)S(6)} %lt.262), kind=kLoop, calls=%fused_computation.22.clone.1 | loop fusion | flops 563200 | bytes 450729 | tf_op jit(solution)/shard_map/while/body/eval_jaxpr/cos | solution.py:42
  118.2 2.7 %subtract_convert_fusion.3 = (bf16[40,32,1408]{2,1,0:T(8,128)(2,1)S(1)}, bf16[40,32,1408]{2,1,0:T(8,128)(2,1)S(1)}) fusion(f32[32,1408]{1,0:T(8,128)S(1)} %get-tuple-element.128, f32[40,1408]{1,0:T(8,128)S(1)} %get-tuple-element.129, f32[32,1408]{1,0:T(8,128)S(1)} %get-tuple-element.130, f32[40,1408]{1,0:T(8,128)S(1)} %get-tuple-element.131), kind=kLoop, calls=%fused_computation.12.clone.1 | loop fusion | flops 16220160 | bytes 8019968 | tf_op jit(solution)/shard_map/convert.3
  120.9 3.4 %maximum_dynamic-update-slice_fusion.2 = bf16[8,2,1280,1408]{3,2,1,0:T(8,128)(2,1)} fusion(bf16[8,2,1280,1408]{3,2,1,0:T(8,128)(2,1)} %get-tuple-element.141, s32[]{:T(128)S(6)} %copy.97, bf16[1,1,1280,1408]{3,2,1,0:T(8,128)(2,1)S(1)} %bitcast.106, bf16[1,1,1280,1408]{3,2,1,0:T(8,128)(2,1)S(1)} %bitcast.105), kind=kLoop, calls=%fused_computation.10.clone.1 | loop fusion | flops 14417920 | bytes 14417924 | tf_op jit(solution)/shard_map/while/body/jit(dynamic_update_index_in_dim)/dynamic_update_slice | solution.py:49
  127.1 2.4 fusion.72
  129.5 3.1 %fusion.73 = (f32[40,1408]{1,0:T(8,128)S(1)}, f32[40,1408]{1,0:T(8,128)S(1)}) fusion(f32[]{:T(128)S(6)} %div.13, s32[]{:T(128)S(6)} %select_n.238, s32[40]{0:T(128)S(1)} %iota_multiply_fusion.7, pred[]{:T(512)S(6)} %lt.262), kind=kLoop, calls=%fused_computation.22.clone.1 | loop fusion | flops 563200 | bytes 450729 | tf_op jit(solution)/shard_map/while/body/eval_jaxpr/cos | solution.py:42
  132.6 2.7 %subtract_convert_fusion.3 = (bf16[40,32,1408]{2,1,0:T(8,128)(2,1)S(1)}, bf16[40,32,1408]{2,1,0:T(8,128)(2,1)S(1)}) fusion(f32[32,1408]{1,0:T(8,128)S(1)} %get-tuple-element.128, f32[40,1408]{1,0:T(8,128)S(1)} %get-tuple-element.129, f32[32,1408]{1,0:T(8,128)S(1)} %get-tuple-element.130, f32[40,1408]{1,0:T(8,128)S(1)} %get-tuple-element.131), kind=kLoop, calls=%fused_computation.12.clone.1 | loop fusion | flops 16220160 | bytes 8019968 | tf_op jit(solution)/shard_map/convert.3
  135.3 3.4 %maximum_dynamic-update-slice_fusion.2 = bf16[8,2,1280,1408]{3,2,1,0:T(8,128)(2,1)} fusion(bf16[8,2,1280,1408]{3,2,1,0:T(8,128)(2,1)} %get-tuple-element.141, s32[]{:T(128)S(6)} %copy.97, bf16[1,1,1280,1408]{3,2,1,0:T(8,128)(2,1)S(1)} %bitcast.106, bf16[1,1,1280,1408]{3,2,1,0:T(8,128)(2,1)S(1)} %bitcast.105), kind=kLoop, calls=%fused_computation.10.clone.1 | loop fusion | flops 14417920 | bytes 14417924 | tf_op jit(solution)/shard_map/while/body/jit(dynamic_update_index_in_dim)/dynamic_update_slice | solution.py:49
  139.7 5.2 %fusion.53 = (f32[4,8,1280]{2,0,1:T(4,128)}, f32[4,8,1280]{2,0,1:T(4,128)}) fusion(f32[8]{0:T(128)S(1)} %convert_divide_fusion, pred[8]{0:T(512)(128)(4,1)S(1)} %broadcast_compare_fusion.2, s32[8]{0:T(128)S(1)} %compare_select_fusion.8, s32[4,1280]{1,0:T(4,128)S(1)} %iota_multiply_fusion.3), kind=kLoop, calls=%fused_computation.75 | loop fusion | flops 368640 | bytes 348232 | tf_op jit(solution)/shard_map/cos | solution.py:56
  144.9 5.5 %all_gather.3 = bf16[8,5632]{1,0:T(8,128)(2,1)S(1)} all-gather(bf16[8,1408]{1,0:T(8,128)(2,1)S(1)} %copy-done.4), channel_id=1, replica_groups=mesh['band'=8,'lon'=4] {'lon'}, dimensions={1}, use_global_device_ids=true | all-gather | bytes 112640 | tf_op jit(solution)/shard_map/all_gather | solution.py:128
  151.4 0.8 copy.86
  152.2 5.9 %gather_fusion.1 = bf16[1280,2,2,8]{3,2,1,0:T(2,128)(2,1)S(1)} fusion(bf16[2,640,2,2,8]{4,3,2,1,0:T(2,128)(2,1)S(1)} %bitcast.111, s32[1280]{0:T(1024)S(1)} %fusion.63), kind=kCustom, calls=%fused_computation.3 | custom fusion | bytes 174080 | tf_op jit(solution)/shard_map/gather | solution.py:126
  158.1 1.4 bitcast_multiply_fusion
  159.5 2.1 fusion.69
  162.9 19.8 %fusion.37 = bf16[2,8,4,1408]{3,2,0,1:T(4,128)(2,1)S(1)} fusion(bf16[8,2,1280,1408]{3,2,1,0:T(8,128)(2,1)} %get-tuple-element.38, bf16[2,4,8,1,1280]{4,1,3,0,2:T(4,128)(2,1)S(1)} %get-tuple-element.94, bf16[2,4,8,1,1280]{4,1,3,0,2:T(4,128)(2,1)S(1)} %get-tuple-element.93, pred[8,4,1408]{2,1,0:T(4,128)(4,1)S(1)} %broadcast_compare_fusion), kind=kOutput, calls=%fused_computation.44 | convolution fusion | flops 462209024 | bytes 58224640 | tf_op jit(solution)/shard_map/fdrtm,rtml->frdl/dot_general | solution.py:85
  182.7 2.1 copy.87
  184.8 3.7 %reshape.805 = bf16[4,2,11264]{2,1,0:T(2,128)(2,1)} reshape(bf16[5632,2,8]{2,1,0:T(2,128)(2,1)S(1)} %bitcast.108) | data formatting | bytes 360448
  188.5 3.6 %all-to-all-start.1 = ((bf16[4,2,11264]{2,1,0:T(2,128)(2,1)}), bf16[4,2,11264]{2,1,0:T(2,128)(2,1)S(1)}, u32[]{:S(2)}, u32[]{:S(2)}) async-start(bf16[4,2,11264]{2,1,0:T(2,128)(2,1)} %reshape.805), calls=%async_computation.1 | async-start | bytes 360448 | tf_op jit(solution)/shard_map/all_to_all | solution.py:134
  192.1 23.8 %fusion.28 = f32[2,4,8,2,1280]{4,1,0,3,2:T(4,128)S(1)} fusion(bf16[8,2,1280,1408]{3,2,1,0:T(8,128)(2,1)} %get-tuple-element.38, bf16[2,8,4,1408]{3,2,0,1:T(4,128)(2,1)S(1)} %fusion.37, f32[8,4,1408]{2,1,0:T(4,128)} %copy.69), kind=kOutput, calls=%fused_computation.41 | convolution fusion | flops 461643776 | bytes 58687488 | tf_op jit(solution)/shard_map/frdl,rtml->fdrtm/dot_general | solution.py:92
  216.5 1.0 copy.74
  217.5 4.9 %gather_fusion.2 = bf16[1280,2,2,8]{3,2,1,0:T(2,128)(2,1)S(1)} fusion(bf16[2,1280,2,8]{3,2,1,0:T(2,128)(2,1)S(1)} %bitcast.112, s32[2048]{0:T(1024)S(1)} %pad_clamp_fusion), kind=kCustom, calls=%fused_computation.4 | custom fusion | bytes 168960 | tf_op jit(solution)/shard_map/gather | solution.py:142
  222.4 1.6 copy.76
  224.0 1.0 copy.77
  225.1 2.0 reshape.807
  227.1 6.0 %all-to-all-start.2 = ((bf16[8,2,2560]{2,1,0:T(2,128)(2,1)}), bf16[8,2,2560]{2,1,0:T(2,128)(2,1)S(1)}, u32[]{:S(2)}, u32[]{:S(2)}) async-start(bf16[8,2,2560]{2,1,0:T(2,128)(2,1)} %reshape.807), calls=%async_computation.2 | async-start | bytes 163840 | tf_op jit(solution)/shard_map/all_to_all | solution.py:145
  233.1 3.4 %reshape.806 = bf16[5632,2,8]{2,1,0:T(2,128)(2,1)S(1)} reshape(bf16[4,2,11264]{2,1,0:T(2,128)(2,1)S(1)} %all-to-all-done.1) | data formatting | bytes 360448
  236.5 4.4 %copy.68 = bf16[4,2,8,1408]{3,2,1,0:T(8,128)(2,1)} copy(bf16[4,2,8,1408]{2,1,3,0:T(2,128)(2,1)S(1)} %bitcast.107) | data formatting | bytes 360448 | tf_op jit(solution)/shard_map/all_to_all | solution.py:134
  240.9 1.5 reshape.808
  242.4 1.1 copy.89
  (82 shorter events, 14.4 us)
Async XLA Ops:
  0.6 2.2 copy-start
  4.7 146.6 %all-to-all-start = ((bf16[2,80,4,64]{1,2,0,3:T(4,128)(2,1)}), bf16[2,80,4,64]{1,2,0,3:T(4,128)(2,1)S(1)}, u32[]{:S(2)}, u32[]{:S(2)}) async-start(bf16[2,80,4,64]{1,2,0,3:T(4,128)(2,1)} %copy.60), calls=%async_computation | async-start | bytes 262144 | tf_op jit(solution)/shard_map/all_to_all | solution.py:124
  23.4 121.5 %copy-start.4 = (bf16[8,1408]{1,0:T(8,128)(2,1)S(1)}, bf16[8,1408]{1,0:T(8,128)(2,1)}, u32[]{:S(2)}) copy-start(bf16[8,1408]{1,0:T(8,128)(2,1)} %param.13) | copy-start | bytes 67588
  159.5 3.2 %copy-start.2 = (f32[4,8,1280]{2,0,1:T(4,128)S(1)}, f32[4,8,1280]{2,0,1:T(4,128)}, u32[]{:S(2)}) copy-start(f32[4,8,1280]{2,0,1:T(4,128)} %get-tuple-element.95) | copy-start | bytes 491524
  159.5 3.2 %copy-start.3 = (f32[4,8,1280]{2,0,1:T(4,128)S(1)}, f32[4,8,1280]{2,0,1:T(4,128)}, u32[]{:S(2)}) copy-start(f32[4,8,1280]{2,0,1:T(4,128)} %get-tuple-element.96) | copy-start | bytes 491524
  188.5 38.6 %all-to-all-start.1 = ((bf16[4,2,11264]{2,1,0:T(2,128)(2,1)}), bf16[4,2,11264]{2,1,0:T(2,128)(2,1)S(1)}, u32[]{:S(2)}, u32[]{:S(2)}) async-start(bf16[4,2,11264]{2,1,0:T(2,128)(2,1)} %reshape.805), calls=%async_computation.1 | async-start | bytes 360448 | tf_op jit(solution)/shard_map/all_to_all | solution.py:134
  227.1 13.8 %all-to-all-start.2 = ((bf16[8,2,2560]{2,1,0:T(2,128)(2,1)}), bf16[8,2,2560]{2,1,0:T(2,128)(2,1)S(1)}, u32[]{:S(2)}, u32[]{:S(2)}) async-start(bf16[8,2,2560]{2,1,0:T(2,128)(2,1)} %reshape.807), calls=%async_computation.2 | async-start | bytes 163840 | tf_op jit(solution)/shard_map/all_to_all | solution.py:145
  233.1 12.1 %copy-start.1 = (bf16[2,80,4,64]{1,3,2,0:T(8,128)(2,1)S(1)}, bf16[2,80,4,64]{1,3,2,0:T(8,128)(2,1)}, u32[]{:S(2)}) copy-start(bf16[2,80,4,64]{1,3,2,0:T(8,128)(2,1)} %param.9) | copy-start | bytes 245764
where the time goes:
time: 246 us; the launch traced here: 245 us
  other arithmetic  108 us (44%)
  local copies, waits for them, and re-layouts  53.3 us (22%)
  matrix products  43.6 us (18%)
  loops' own time  17 us (7%)
  starting transfers between devices  16.9 us (7%)
  blocking collectives  5.51 us (2%)
    dynamic_update_slice x8, other arithmetic, cycle_table(): return lax.map(single_period, lengths)  27.7 us
    cos x8, other arithmetic, single_period(): cos_coarse, sin_coarse = (jnp.cos(coarse), jnp.sin(coarse))  24.5 us
    dot_general x1, matrix products, analyze(): jnp.einsum('frdl,rtml->fdrtm', values, tables, preferred_element_type=jnp...  23.8 us
    another operation x11, other arithmetic  23.2 us
    dot_general x1, matrix products, synthesize(): jnp.einsum('fdrtm,rtml->frdl', coeffs, tables, preferred_element_type=jnp...  19.8 us
    sin x8, other arithmetic, single_period(): cos_fine, sin_fine = (jnp.cos(fine), jnp.sin(fine))  19.3 us
    another operation x1, loops' own time, cycle_table(): return lax.map(single_period, lengths)  17 us
    unnamed x18, local copies, waits for them, and re-layouts  11.5 us
  transfers between devices with their start and end apart: 3, of which 0 were waited for; matrix products, arithmetic and copies ran while one was open for 65% of the time, Pallas kernels for 0%

commit v1 on v0

v1 whole, which is shorter than its diff:
```python
import functools
import math

import jax
import jax.numpy as jnp
import numpy as np
from jax import lax
from jax.experimental import pallas as pl
from jax.experimental.pallas import tpu as pltpu
from jax.sharding import PartitionSpec as P

TWO_PI = 2.0 * math.pi
LANES = 128
CHUNK = 256
AXES = ("band", "lon")


def cos_sin(product, length, inverse):
    turns = jnp.floor(product * inverse + 0.5)
    half = (product - turns * length) * (inverse * (0.5 * TWO_PI))
    square = half * half
    sine = jnp.full_like(half, -1.0 / math.factorial(11))
    for order in (9, 7, 5, 3, 1):
        sine = sine * square + (-1.0) ** (order // 2) / math.factorial(order)
    sine = sine * half
    cosine = jnp.full_like(half, 1.0 / math.factorial(12))
    for order in (10, 8, 6, 4, 2, 0):
        cosine = cosine * square + (-1.0) ** (order // 2) / math.factorial(order)
    return 1.0 - 2.0 * sine * sine, 2.0 * sine * cosine


def row_kernel(
    slot_count,
    length_ref,
    wave_band_ref,
    pair_band_ref,
    spec_ref,
    factor_ref,
    grid_ref,
    out_ref,
    hot,
    lhs,
    total,
    cos_state,
    sin_state,
    cos_step,
    sin_step,
    cos_high,
    sin_high,
    cos_high_step,
    sin_high_step,
):
    row = pl.program_id(0)
    fields = spec_ref.shape[2]
    slots, waves = hot.shape
    pairs = pair_band_ref.shape[0]
    high = waves // LANES

    @pl.when(row == 0)
    def _():
        wave = lax.broadcasted_iota(jnp.int32, (1, waves), 1)
        pair_of_wave = jnp.minimum(wave, waves - 1 - wave)
        wave_band = wave_band_ref[...]
        before = jnp.zeros((1, waves), jnp.int32)
        for start in range(0, pairs, 128):
            size = min(128, pairs - start)
            pair = lax.broadcasted_iota(jnp.int32, (size, waves), 0) + start
            same = (pair_band_ref[start : start + size, :] == wave_band) & (pair < pair_of_wave)
            before = before + jnp.sum(same.astype(jnp.int32), axis=0, keepdims=True)
        slot_of_wave = wave_band * slot_count + before
        for start in range(0, slots, 32):
            slot = lax.broadcasted_iota(jnp.int32, (32, waves), 0) + start
            hot[start : start + 32, :] = jnp.where(slot == slot_of_wave, 1.0, 0.0).astype(
                jnp.bfloat16
            )

    n = length_ref[row]
    length = jnp.full((1, 1), n, jnp.int32).astype(jnp.float32)
    inverse = 1.0 / length
    norm = lax.rsqrt(length)

    wave = lax.broadcasted_iota(jnp.int32, (1, waves), 1)
    kept = jnp.where(2 * wave < n, 1.0, 0.0)
    weight = kept * jnp.where(wave == 0, 1.0, 2.0)
    half = waves // 2
    for t in range(2):
        pieces = []
        for member in range(2):
            pieces.append(
                jnp.dot(
                    spec_ref[0, 2 * member + t],
                    hot[:, member * half : (member + 1) * half],
                    preferred_element_type=jnp.float32,
                )
            )
        ordered = (jnp.concatenate(pieces, axis=1) * weight).astype(jnp.bfloat16)
        for b in range(high):
            part = ordered[:, b * LANES : (b + 1) * LANES]
            if t == 0:
                lhs[b * fields : (b + 1) * fields, 0:LANES] = part
                lhs[(high + b) * fields : (high + b + 1) * fields, LANES : 2 * LANES] = -part
            else:
                lhs[b * fields : (b + 1) * fields, LANES : 2 * LANES] = part
                lhs[(high + b) * fields : (high + b + 1) * fields, 0:LANES] = part

    low_wave = lax.broadcasted_iota(jnp.int32, (LANES, CHUNK), 0).astype(jnp.float32)
    place = lax.broadcasted_iota(jnp.int32, (LANES, CHUNK), 1).astype(jnp.float32)
    cos_state[...], sin_state[...] = cos_sin(low_wave * place, length, inverse)
    step_wave = lax.broadcasted_iota(jnp.int32, (LANES, LANES), 0).astype(jnp.float32)
    cos_step[...], sin_step[...] = cos_sin(step_wave * float(CHUNK), length, inverse)
    padded = cos_high.shape[0]
    high_wave = LANES * lax.broadcasted_iota(jnp.int32, (padded, CHUNK), 0)
    high_place = lax.broadcasted_iota(jnp.int32, (padded, CHUNK), 1)
    cos_high[...], sin_high[...] = cos_sin(
        (high_wave * high_place).astype(jnp.float32), length, inverse
    )
    cos_high_step[...], sin_high_step[...] = cos_sin(
        (high_wave * CHUNK).astype(jnp.float32), length, inverse
    )
    total[...] = jnp.zeros_like(total)
    grid_ref[...] = jnp.zeros_like(grid_ref)

    def chunk(h, carry):
        columns = pl.ds(pl.multiple_of(h * CHUNK, CHUNK), CHUNK)
        cosine, sine = cos_state[...], sin_state[...]
        table = jnp.concatenate([cosine, -sine], axis=0).astype(jnp.bfloat16)
        found = jnp.dot(lhs[...], table, preferred_element_type=jnp.float32)
        high_cos, high_sin = cos_high[...], sin_high[...]
        value = jnp.zeros((fields, CHUNK), jnp.float32)
        for b in range(high):
            real = found[b * fields : (b + 1) * fields]
            imag = found[(high + b) * fields : (high + b + 1) * fields]
            value = value + (real * high_cos[b : b + 1] - imag * high_sin[b : b + 1])
        at = h * CHUNK + lax.broadcasted_iota(jnp.int32, (1, CHUNK), 1)
        value = jnp.where(at < n, value * norm, 0.0).astype(jnp.bfloat16)
        grid_ref[0, :, columns] = value
        product = factor_ref[0, :, columns].astype(jnp.float32) * value.astype(jnp.float32)
        product = product.astype(jnp.bfloat16).astype(jnp.float32)
        turned = [product * high_cos[b : b + 1] for b in range(high)]
        turned += [product * (-high_sin[b : b + 1]) for b in range(high)]
        turned = jnp.concatenate(turned, axis=0).astype(jnp.bfloat16)
        total[...] += lax.dot_general(
            turned, table, (((1,), (1,)), ((), ())), preferred_element_type=jnp.float32
        )
        step_cos = jnp.concatenate([cos_step[...]] * (CHUNK // LANES), axis=1)
        step_sin = jnp.concatenate([sin_step[...]] * (CHUNK // LANES), axis=1)
        cos_state[...] = cosine * step_cos - sine * step_sin
        sin_state[...] = sine * step_cos + cosine * step_sin
        high_step_cos, high_step_sin = cos_high_step[...], sin_high_step[...]
        cos_high[...] = high_cos * high_step_cos - high_sin * high_step_sin
        sin_high[...] = high_sin * high_step_cos + high_cos * high_step_sin
        return carry

    lax.fori_loop(0, (n + CHUNK - 1) // CHUNK, chunk, 0)

    scale = kept * norm
    for t in range(2):
        pieces = []
        for b in range(high):
            real = slice(b * fields, (b + 1) * fields)
            imag = slice((high + b) * fields, (high + b + 1) * fields)
            if t == 0:
                pieces.append(total[real, 0:LANES] - total[imag, LANES : 2 * LANES])
            else:
                pieces.append(total[imag, 0:LANES] + total[real, LANES : 2 * LANES])
        finished = (jnp.concatenate(pieces, axis=1) * scale).astype(jnp.bfloat16)
        for member in range(2):
            out_ref[0, 2 * member + t] = lax.dot_general(
                finished[:, member * half : (member + 1) * half],
                hot[:, member * half : (member + 1) * half],
                (((1,), (1,)), ((), ())),
                preferred_element_type=jnp.float32,
            ).astype(jnp.bfloat16)


def transform_rows(lengths, pair_band, spec, factor, slot_count):
    rows, _, fields, slots = spec.shape
    points = factor.shape[2]
    pairs = pair_band.shape[0]
    waves = 2 * pairs
    high = waves // LANES
    padded = -(-high // 8) * 8
    stacked = 2 * high * fields
    wave_band = jnp.concatenate([pair_band, pair_band[::-1]])[None, :]
    grid_spec = pltpu.PrefetchScalarGridSpec(
        num_scalar_prefetch=1,
        grid=(rows,),
        in_specs=[
            pl.BlockSpec((1, waves), lambda i, *_: (0, 0)),
            pl.BlockSpec((pairs, 1), lambda i, *_: (0, 0)),
            pl.BlockSpec((1, 4, fields, slots), lambda i, *_: (i, 0, 0, 0)),
            pl.BlockSpec((1, 1, points), lambda i, *_: (i, 0, 0)),
        ],
        out_specs=[
            pl.BlockSpec((1, fields, points), lambda i, *_: (i, 0, 0)),
            pl.BlockSpec((1, 4, fields, slots), lambda i, *_: (i, 0, 0, 0)),
        ],
        scratch_shapes=[
            pltpu.VMEM((slots, waves), jnp.bfloat16),
            pltpu.VMEM((stacked, 2 * LANES), jnp.bfloat16),
            pltpu.VMEM((stacked, 2 * LANES), jnp.float32),
            pltpu.VMEM((LANES, CHUNK), jnp.float32),
            pltpu.VMEM((LANES, CHUNK), jnp.float32),
            pltpu.VMEM((LANES, LANES), jnp.float32),
            pltpu.VMEM((LANES, LANES), jnp.float32),
            pltpu.VMEM((padded, CHUNK), jnp.float32),
            pltpu.VMEM((padded, CHUNK), jnp.float32),
            pltpu.VMEM((padded, CHUNK), jnp.float32),
            pltpu.VMEM((padded, CHUNK), jnp.float32),
        ],
    )
    return pl.pallas_call(
        functools.partial(row_kernel, slot_count),
        grid_spec=grid_spec,
        out_shape=[
            jax.ShapeDtypeStruct((rows, fields, points), jnp.bfloat16),
            jax.ShapeDtypeStruct((rows, 4, fields, slots), jnp.bfloat16),
        ],
        compiler_params=pltpu.CompilerParams(dimension_semantics=("arbitrary",)),
    )(lengths, wave_band, pair_band[:, None], spec, factor)


def on_device(coefficients, cycle_length, row_latitude, pair_band, gridpoint_factor):
    bands, lanes = lax.axis_size("band"), lax.axis_size("lon")
    device = lax.axis_index("band") * lanes + lax.axis_index("lon")
    own_fields, slot_count, parts, latitudes = coefficients.shape
    band_rows, points = gridpoint_factor.shape
    fields = own_fields * lanes
    own_rows = -(-band_rows // lanes)
    lane_rows = np.arange(lanes * own_rows)
    inside = np.tile(lane_rows < band_rows, bands)
    clamped = np.minimum(lane_rows, band_rows - 1)
    row_ids = (np.arange(bands)[:, None] * band_rows + clamped[None, :]).reshape(-1)
    held = row_latitude if inside.all() else jnp.take(row_latitude, row_ids)
    onehot = held[:, None] == jnp.arange(latitudes, dtype=jnp.int32)[None, :]
    own = lax.dynamic_slice_in_dim(held, device * own_rows, own_rows)
    lengths = jnp.take(cycle_length, own)

    leaving = jnp.einsum(
        "rl,fstl->rtfs",
        onehot.astype(jnp.bfloat16),
        coefficients,
        preferred_element_type=jnp.float32,
    ).astype(jnp.bfloat16)
    arrived = lax.all_to_all(leaving, AXES, split_axis=0, concat_axis=0, tiled=True)
    arrived = arrived.reshape(bands, lanes, own_rows, parts, own_fields, slot_count)
    spec = jnp.transpose(arrived, (2, 3, 1, 4, 0, 5)).reshape(
        own_rows, parts, fields, bands * slot_count
    )
    factor = gridpoint_factor if inside.all() else jnp.take(gridpoint_factor, clamped, axis=0)
    factor = lax.all_to_all(factor, "lon", split_axis=0, concat_axis=1, tiled=True)

    grid, result = transform_rows(lengths, pair_band, spec, factor[:, None, :], slot_count)

    grid_rows = lax.all_to_all(grid, "lon", split_axis=2, concat_axis=0, tiled=True)
    grid_rows = jnp.transpose(grid_rows, (1, 0, 2))[:, :band_rows]

    result = result.reshape(own_rows, parts, lanes, own_fields, bands, slot_count)
    result = jnp.transpose(result, (4, 2, 0, 1, 3, 5)).reshape(
        bands * lanes * own_rows, parts, own_fields, slot_count
    )
    returned = lax.all_to_all(result, AXES, split_axis=0, concat_axis=0, tiled=True)
    back = onehot & inside[:, None]
    tendencies = jnp.einsum(
        "rtfs,rl->fstl",
        returned,
        back.astype(jnp.bfloat16),
        preferred_element_type=jnp.float32,
    ).astype(jnp.bfloat16)
    return (grid_rows, tendencies)


def solution(mesh):
    return jax.shard_map(
        on_device,
        mesh=mesh,
        in_specs=(P("lon", "band", None, None), P(), P(), P(), P("band", "lon")),
        out_specs=(P(None, "band", "lon"), P("lon", "band", None, None)),
        check_vma=False,
    )
```

time: 246 us -> 78.3 us (0.32)
  other arithmetic: 108 us -> 2.73 us
  matrix products: 43.6 us -> 1.05 us
  local copies, waits for them, and re-layouts: 53.3 us -> 24.4 us
  loops' own time: 17 us -> 0 us
  waiting for transfers between devices: 0.01 us -> 12.7 us
  Pallas kernels: 0 us -> 9.31 us
  starting transfers between devices: 16.9 us -> 26.2 us
  blocking collectives: 5.51 us -> 0 us
    dot_general x2, matrix products: 43.6 us -> 1.05 us  [the longest x1 0.88 us: on_device(): jnp.einsum('rl,fstl->rtfs', onehot.astype(jnp.bfloat16), coefficients, pr...]
    cos x9 -> x0, other arithmetic: 29.7 us -> none  [the longest x8 24.5 us: single_period(): cos_coarse, sin_coarse = (jnp.cos(coarse), jnp.sin(coarse))]
    dynamic_update_slice x8 -> x0, other arithmetic: 27.7 us -> none  [cycle_table(): return lax.map(single_period, lengths)]
    another operation x11 -> x0, other arithmetic: 23.2 us -> none
    sin x8 -> x0, other arithmetic: 19.3 us -> none  [single_period(): cos_fine, sin_fine = (jnp.cos(fine), jnp.sin(fine))]
    another operation x1 -> x0, loops' own time: 17 us -> none  [cycle_table(): return lax.map(single_period, lengths)]
    gather x6 -> x1, local copies, waits for them, and re-layouts: 15.4 us -> 1.29 us  [on_device(): lengths = jnp.take(cycle_length, own)]
    all_to_all x3 -> x4, waiting for transfers between devices: 0.01 us -> 12.7 us  [the longest x1 6.25 us: on_device(): lax.all_to_all(leaving, AXES, split_axis=0, concat_axis=0, tiled=True)]
  transfers between devices with their start and end apart: 3 -> 4, of which waited for: 0 -> 3; matrix products, arithmetic and copies ran while one was open for 65% -> 20% of each run, Pallas kernels for 0% -> 0%
where the time goes in v1:
time: 78.3 us; the launch traced here: 77.1 us
  starting transfers between devices  26.2 us (33%)
  local copies, waits for them, and re-layouts  24.4 us (31%)
  waiting for transfers between devices  12.7 us (16%)
  Pallas kernels  9.31 us (12%)
  other arithmetic  2.73 us (3%)
  matrix products  1.05 us (1%)
    all_to_all x1, starting transfers between devices, on_device(): lax.all_to_all(grid, 'lon', split_axis=2, concat_axis=0, tiled=True)  10.3 us
    pallas_call x1, Pallas kernels, transform_rows(): pl.pallas_call(functools.partial(row_kernel, slot_count), grid_spec=grid_...  9.31 us
    unnamed x9, local copies, waits for them, and re-layouts  7.78 us
    all_to_all x1, starting transfers between devices, on_device(): lax.all_to_all(leaving, AXES, split_axis=0, concat_axis=0, tiled=True)  6.8 us
    all_to_all x1, waiting for transfers between devices, on_device(): lax.all_to_all(leaving, AXES, split_axis=0, concat_axis=0, tiled=True)  6.25 us
    pallas_call x1, local copies, waits for them, and re-layouts, transform_rows(): pl.pallas_call(functools.partial(row_kernel, slot_count), grid_spec=grid_...  5.31 us
    all_to_all x1, starting transfers between devices, on_device(): lax.all_to_all(result, AXES, split_axis=0, concat_axis=0, tiled=True)  4.81 us
    all_to_all x1, starting transfers between devices, on_device(): lax.all_to_all(factor, 'lon', split_axis=0, concat_axis=1, tiled=True)  4.26 us
  transfers between devices with their start and end apart: 4, of which 3 were waited for; matrix products, arithmetic and copies ran while one was open for 20% of the time, Pallas kernels for 0%

profile of v1, /device:TPU:0, one launch (start us, length us, event | category | flops | bytes accessed | tf_op | source)
XLA Modules:
  0.0 77.1 jit_solution(9990997030161271466)
XLA Ops:
  0.6 0.0 copy-start
  0.6 1.4 %all_to_all.32 = bf16[4,2,1408]{2,1,0:T(2,128)(2,1)} reshape(bf16[8,1408]{1,0:T(8,128)(2,1)} %param.10) | data formatting | bytes 45056 | tf_op jit(solution)/shard_map/all_to_all | solution.py:251
  2.0 4.3 %all-to-all-start.1 = ((bf16[4,2,1408]{2,1,0:T(2,128)(2,1)}), bf16[4,2,1408]{2,1,0:T(2,128)(2,1)S(1)}, u32[]{:S(2)}, u32[]{:S(2)}) async-start(bf16[4,2,1408]{2,1,0:T(2,128)(2,1)} %all_to_all.32), calls=%async_computation.1 | async-start | bytes 45056 | tf_op jit(solution)/shard_map/all_to_all | solution.py:251
  6.3 0.7 compare_select_fusion
  7.0 0.0 copy-done
  7.0 0.9 %fusion = bf16[64,4,2,80]{3,0,1,2:T(8,128)(2,1)S(1)} fusion(bf16[2,80,4,64]{1,3,2,0:T(8,128)(2,1)S(1)} %copy-done, s32[64]{0:T(128)} %param.8), kind=kOutput, calls=%fused_computation.3 | convolution fusion | flops 5287936 | bytes 164096 | tf_op jit(solution)/shard_map/rl,fstl->rtfs/dot_general | solution.py:239
  7.9 0.8 rev.3
  8.7 0.7 pad_add_fusion
  9.4 1.6 %broadcast_in_dim.19.pair_band_ref = s32[640,1]{1,0:T(8,128)} reshape(s32[640]{0:T(1024)} %param.9) | data formatting | bytes 5120 | tf_op jit(solution)/shard_map/broadcast_in_dim | solution.py:220
  11.0 0.8 copy.23
  11.7 0.6 broadcast_in_dim.16.wave_band_ref
  12.3 1.3 %gather_fusion = s32[2]{0:T(128)S(1)} fusion(s32[64]{0:T(128)} %param.7, s32[1024]{0:T(1024)S(1)} %pad_clamp_fusion), kind=kCustom, calls=%fused_computation | custom fusion | bytes 24 | tf_op jit(solution)/shard_map/jit(_take)/gather | solution.py:237
  13.6 0.0 all-to-all-done.1
  13.6 6.8 %all-to-all-start = ((bf16[64,4,2,80]{3,1,2,0:T(4,128)(2,1)}), bf16[64,4,2,80]{3,1,2,0:T(4,128)(2,1)S(1)}, u32[]{:S(2)}, u32[]{:S(2)}) async-start(bf16[64,4,2,80]{3,1,2,0:T(4,128)(2,1)} %copy.23), calls=%async_computation | async-start | bytes 262144 | tf_op jit(solution)/shard_map/all_to_all | solution.py:245
  20.4 1.3 %and_select_fusion.length_ref = s32[2]{0:T(128)} fusion(s32[2]{0:T(128)S(1)} %gather_fusion, s32[64]{0:T(128)} %param.8, s32[]{:T(128)S(6)} %select_n.12), kind=kLoop, calls=%fused_computation.14 | loop fusion | flops 14 | bytes 28 | tf_op jit(solution)/shard_map/jit(_take)/select_n | solution.py:237
  21.7 0.7 copy.26.factor_ref
  22.3 6.2 %all-to-all-done = bf16[64,4,2,80]{3,1,2,0:T(4,128)(2,1)S(1)} async-done(((bf16[64,4,2,80]{3,1,2,0:T(4,128)(2,1)}), bf16[64,4,2,80]{3,1,2,0:T(4,128)(2,1)S(1)}, u32[]{:S(2)}, u32[]{:S(2)}) %all-to-all-start) | async-done | bytes 81952 | tf_op jit(solution)/shard_map/all_to_all | solution.py:245
  28.6 0.1 copy.38
  28.7 0.8 %reshape.27.spec_ref = bf16[2,4,8,640]{3,2,1,0:T(8,128)(2,1)} reshape(bf16[2,4,4,2,8,80]{5,4,3,2,1,0:T(8,128)(2,1)S(1)} %bitcast.36) | data formatting | bytes 163840 | tf_op jit(solution)/shard_map/reshape | solution.py:247
  29.5 9.3 %shard_map.77 = (bf16[2,8,5632]{2,1,0:T(8,128)(2,1)}, bf16[2,4,8,640]{3,2,1,0:T(8,128)(2,1)}) custom-call(s32[2]{0:T(128)} %and_select_fusion.length_ref, s32[1,1280]{1,0:T(1,128)} %broadcast_in_dim.16.wave_band_ref, s32[640,1]{1,0:T(8,128)} %broadcast_in_dim.19.pair_band_ref, bf16[2,4,8,640]{3,2,1,0:T(8,128)(2,1)} %reshape.27.spec_ref, ...), custom_call_target="tpu_custom_call" | custom-call | tf_op jit(solution)/shard_map/pallas_call | solution.py:212
  38.8 0.0 copy-start.1
  38.8 5.3 %copy.27 = bf16[2,8,5632]{1,0,2:T(2,128)(2,1)S(1)} copy(bf16[2,8,5632]{2,1,0:T(8,128)(2,1)} %get-tuple-element.4) | data formatting | bytes 360448 | tf_op jit(solution)/shard_map/pallas_call | solution.py:212
  44.1 3.7 %reshape.41 = bf16[4,2,11264]{2,1,0:T(2,128)(2,1)} reshape(bf16[5632,2,8]{2,1,0:T(2,128)(2,1)S(1)} %bitcast.33) | data formatting | bytes 360448
  47.8 10.3 %all-to-all-start.2 = ((bf16[4,2,11264]{2,1,0:T(2,128)(2,1)}), bf16[4,2,11264]{2,1,0:T(2,128)(2,1)S(1)}, u32[]{:S(2)}, u32[]{:S(2)}) async-start(bf16[4,2,11264]{2,1,0:T(2,128)(2,1)} %reshape.41), calls=%async_computation.2 | async-start | bytes 360448 | tf_op jit(solution)/shard_map/all_to_all | solution.py:255
  58.1 0.0 copy-done.1
  58.1 0.2 reshape.28
  58.3 0.8 copy.29
  59.0 4.2 %all-to-all-done.2 = bf16[4,2,11264]{2,1,0:T(2,128)(2,1)S(1)} async-done(((bf16[4,2,11264]{2,1,0:T(2,128)(2,1)}), bf16[4,2,11264]{2,1,0:T(2,128)(2,1)S(1)}, u32[]{:S(2)}, u32[]{:S(2)}) %all-to-all-start.2) | async-done | bytes 180256 | tf_op jit(solution)/shard_map/all_to_all | solution.py:255
  63.2 4.8 %all-to-all-start.3 = ((bf16[64,4,2,80]{3,2,1,0:T(2,128)(2,1)}), bf16[64,4,2,80]{3,2,1,0:T(2,128)(2,1)S(1)}, u32[]{:S(2)}, u32[]{:S(2)}) async-start(bf16[64,4,2,80]{3,2,1,0:T(2,128)(2,1)} %bitcast.12), calls=%async_computation.3 | async-start | bytes 262144 | tf_op jit(solution)/shard_map/all_to_all | solution.py:262
  68.1 0.0 copy-start.2
  68.1 3.4 %reshape.42 = bf16[5632,2,8]{2,1,0:T(2,128)(2,1)S(1)} reshape(bf16[4,2,11264]{2,1,0:T(2,128)(2,1)S(1)} %all-to-all-done.2) | data formatting | bytes 360448
  71.5 1.8 %copy.28 = bf16[4,2,8,1408]{3,1,0,2:T(2,128)(2,1)S(1)} copy(bf16[4,2,8,1408]{2,1,3,0:T(2,128)(2,1)S(1)} %bitcast.34) | data formatting | bytes 360448 | tf_op jit(solution)/shard_map/all_to_all | solution.py:255
  73.3 0.7 all_to_all.38
  74.0 2.3 %all-to-all-done.3 = bf16[64,4,2,80]{3,2,1,0:T(2,128)(2,1)S(1)} async-done(((bf16[64,4,2,80]{3,2,1,0:T(2,128)(2,1)}), bf16[64,4,2,80]{3,2,1,0:T(2,128)(2,1)S(1)}, u32[]{:S(2)}, u32[]{:S(2)}) %all-to-all-start.3) | async-done | bytes 81952 | tf_op jit(solution)/shard_map/all_to_all | solution.py:262
  76.3 0.0 copy-done.2
  76.3 0.2 fusion.1
  76.5 0.7 copy.31
  (1 shorter events, 0.0 us)
Async XLA Ops:
  0.6 6.4 %copy-start = (bf16[2,80,4,64]{1,3,2,0:T(8,128)(2,1)S(1)}, bf16[2,80,4,64]{1,3,2,0:T(8,128)(2,1)}, u32[]{:S(2)}) copy-start(bf16[2,80,4,64]{1,3,2,0:T(8,128)(2,1)} %param.6) | copy-start | bytes 245764
  2.0 11.5 %all-to-all-start.1 = ((bf16[4,2,1408]{2,1,0:T(2,128)(2,1)}), bf16[4,2,1408]{2,1,0:T(2,128)(2,1)S(1)}, u32[]{:S(2)}, u32[]{:S(2)}) async-start(bf16[4,2,1408]{2,1,0:T(2,128)(2,1)} %all_to_all.32), calls=%async_computation.1 | async-start | bytes 45056 | tf_op jit(solution)/shard_map/all_to_all | solution.py:251
  13.6 15.0 %all-to-all-start = ((bf16[64,4,2,80]{3,1,2,0:T(4,128)(2,1)}), bf16[64,4,2,80]{3,1,2,0:T(4,128)(2,1)S(1)}, u32[]{:S(2)}, u32[]{:S(2)}) async-start(bf16[64,4,2,80]{3,1,2,0:T(4,128)(2,1)} %copy.23), calls=%async_computation | async-start | bytes 262144 | tf_op jit(solution)/shard_map/all_to_all | solution.py:245
  38.8 19.3 %copy-start.1 = (bf16[2,4,8,640]{3,2,1,0:T(8,128)(2,1)S(1)}, bf16[2,4,8,640]{3,2,1,0:T(8,128)(2,1)}, u32[]{:S(2)}) copy-start(bf16[2,4,8,640]{3,2,1,0:T(8,128)(2,1)} %get-tuple-element.5) | copy-start | bytes 245764
  47.8 15.4 %all-to-all-start.2 = ((bf16[4,2,11264]{2,1,0:T(2,128)(2,1)}), bf16[4,2,11264]{2,1,0:T(2,128)(2,1)S(1)}, u32[]{:S(2)}, u32[]{:S(2)}) async-start(bf16[4,2,11264]{2,1,0:T(2,128)(2,1)} %reshape.41), calls=%async_computation.2 | async-start | bytes 360448 | tf_op jit(solution)/shard_map/all_to_all | solution.py:255
  63.2 13.0 %all-to-all-start.3 = ((bf16[64,4,2,80]{3,2,1,0:T(2,128)(2,1)}), bf16[64,4,2,80]{3,2,1,0:T(2,128)(2,1)S(1)}, u32[]{:S(2)}, u32[]{:S(2)}) async-start(bf16[64,4,2,80]{3,2,1,0:T(2,128)(2,1)} %bitcast.12), calls=%async_computation.3 | async-start | bytes 262144 | tf_op jit(solution)/shard_map/all_to_all | solution.py:262
  68.1 8.2 %copy-start.2 = (s32[64]{0:T(128)S(1)}, s32[64]{0:T(128)}, u32[]{:S(2)}) copy-start(s32[64]{0:T(128)} %param.8) | copy-start | bytes 772

commit v2 on v1

v2 whole, which is shorter than its diff:
```python
import functools
import math

import jax
import jax.numpy as jnp
import numpy as np
from jax import lax
from jax.experimental import pallas as pl
from jax.experimental.pallas import tpu as pltpu
from jax.sharding import PartitionSpec as P

TWO_PI = 2.0 * math.pi
LANES = 128
CHUNK = 256


def cos_sin(product, length, inverse):
    turns = jnp.floor(product * inverse + 0.5)
    half = (product - turns * length) * (inverse * (0.5 * TWO_PI))
    square = half * half
    sine = jnp.full_like(half, -1.0 / math.factorial(11))
    for order in (9, 7, 5, 3, 1):
        sine = sine * square + (-1.0) ** (order // 2) / math.factorial(order)
    sine = sine * half
    cosine = jnp.full_like(half, 1.0 / math.factorial(12))
    for order in (10, 8, 6, 4, 2, 0):
        cosine = cosine * square + (-1.0) ** (order // 2) / math.factorial(order)
    return 1.0 - 2.0 * sine * sine, 2.0 * sine * cosine


MESH = pl.DeviceIdType.MESH


def greet(devices, lanes, me):
    barrier = pltpu.get_barrier_semaphore()

    def signal(k, carry):
        flat = lax.rem(me + k, devices)
        peer = {"band": flat // lanes, "lon": lax.rem(flat, lanes)}
        pl.semaphore_signal(barrier, inc=1, device_id=peer, device_id_type=MESH)
        return carry

    lax.fori_loop(1, devices, signal, 0)
    pl.semaphore_wait(barrier, devices - 1)


def send_chunks(devices, lanes, me, source, target, send_sem, recv_sem):
    def send(k, carry):
        flat = lax.rem(me + k, devices)
        pltpu.make_async_remote_copy(
            src_ref=source.at[flat],
            dst_ref=target.at[me],
            send_sem=send_sem,
            recv_sem=recv_sem,
            device_id={"band": flat // lanes, "lon": lax.rem(flat, lanes)},
            device_id_type=MESH,
        ).start()
        return carry

    lax.fori_loop(1, devices, send, 0)
    target[me] = source[me]


def wait_chunks(devices, lanes, source, target, send_sem, recv_sem):
    pltpu.make_async_remote_copy(
        src_ref=source.at[pl.ds(0, devices - 1)],
        dst_ref=target.at[pl.ds(0, devices - 1)],
        send_sem=send_sem,
        recv_sem=recv_sem,
        device_id={"band": lax.axis_index("band"), "lon": lax.axis_index("lon")},
        device_id_type=MESH,
    ).wait()


def gather_kernel(
    bands, lanes, leaving, factor, arrived, cycles, send_sem, recv_sem, row_send_sem, row_recv_sem
):
    lane = lax.axis_index("lon")
    me = lax.axis_index("band") * lanes + lane
    devices = bands * lanes
    points = factor.shape[1]
    greet(devices, lanes, me)
    copies = []
    for j in range(1, lanes):
        own = pl.ds(pl.multiple_of(lane * points, LANES), points)
        copies.append(
            pltpu.make_async_remote_copy(
                src_ref=factor,
                dst_ref=cycles.at[:, own],
                send_sem=row_send_sem.at[j],
                recv_sem=row_recv_sem.at[j],
                device_id={"lon": lax.rem(lane + j, lanes)},
                device_id_type=MESH,
            )
        )
        copies[-1].start()
    send_chunks(devices, lanes, me, leaving, arrived, send_sem, recv_sem)
    cycles[:, pl.ds(pl.multiple_of(lane * points, LANES), points)] = factor[...]
    for copy in copies:
        copy.wait()
    wait_chunks(devices, lanes, leaving, arrived, send_sem, recv_sem)


def scatter_kernel(
    bands, lanes, grid, leaving, blocks, arrived, send_sem, recv_sem, row_send_sem, row_recv_sem
):
    lane = lax.axis_index("lon")
    me = lax.axis_index("band") * lanes + lane
    devices = bands * lanes
    points = grid.shape[2] // lanes
    greet(devices, lanes, me)
    copies = []
    for j in range(1, lanes):
        other = lax.rem(lane + j, lanes)
        copies.append(
            pltpu.make_async_remote_copy(
                src_ref=grid.at[:, :, pl.ds(pl.multiple_of(other * points, LANES), points)],
                dst_ref=blocks.at[lane],
                send_sem=row_send_sem.at[j],
                recv_sem=row_recv_sem.at[j],
                device_id={"lon": other},
                device_id_type=MESH,
            )
        )
        copies[-1].start()
    send_chunks(devices, lanes, me, leaving, arrived, send_sem, recv_sem)
    blocks[lane] = grid[:, :, pl.ds(pl.multiple_of(lane * points, LANES), points)]
    for copy in copies:
        copy.wait()
    wait_chunks(devices, lanes, leaving, arrived, send_sem, recv_sem)


def exchange(kernel, bands, lanes, collective_id, out_shape, first, second):
    return pl.pallas_call(
        functools.partial(kernel, bands, lanes),
        out_shape=out_shape,
        in_specs=[pl.BlockSpec(memory_space=pltpu.VMEM)] * 2,
        out_specs=[pl.BlockSpec(memory_space=pltpu.VMEM)] * 2,
        scratch_shapes=[
            pltpu.SemaphoreType.DMA,
            pltpu.SemaphoreType.DMA,
            pltpu.SemaphoreType.DMA((lanes,)),
            pltpu.SemaphoreType.DMA((lanes,)),
        ],
        compiler_params=pltpu.CompilerParams(collective_id=collective_id, has_side_effects=True),
    )(first, second)


def row_kernel(
    lanes,
    band_rows,
    order_ref,
    scalars_ref,
    wave_band_ref,
    pair_band_ref,
    arrived_ref,
    factor_ref,
    grid_ref,
    out_ref,
    hot,
    ordered,
    finished,
    lhs,
    total,
    row_factor,
    cos_state,
    sin_state,
    cos_step,
    sin_step,
    cos_high,
    sin_high,
    cos_high_step,
    sin_high_step,
):
    rows, fields = grid_ref.shape[0], grid_ref.shape[1]
    slots, waves = hot.shape
    devices = arrived_ref.shape[0]
    bands = devices // lanes
    pairs = pair_band_ref.shape[0]
    high = waves // LANES
    half = waves // 2
    stacked = arrived_ref.shape[1] * lanes

    wave = lax.broadcasted_iota(jnp.int32, (1, waves), 1)
    pair_of_wave = jnp.minimum(wave, waves - 1 - wave)
    wave_band = wave_band_ref[...]
    before = jnp.zeros((1, waves), jnp.int32)
    for start in range(0, pairs, 128):
        size = min(128, pairs - start)
        pair = lax.broadcasted_iota(jnp.int32, (size, waves), 0) + start
        same = (pair_band_ref[start : start + size, :] == wave_band) & (pair < pair_of_wave)
        before = before + jnp.sum(same.astype(jnp.int32), axis=0, keepdims=True)
    slot_of_wave = wave_band * LANES + before

    def fill(step, carry):
        start = pl.multiple_of(step * 32, 32)
        slot = lax.broadcasted_iota(jnp.int32, (32, waves), 0) + start
        hot[pl.ds(start, 32), :] = jnp.where(slot == slot_of_wave, 1.0, 0.0).astype(jnp.bfloat16)
        return carry

    lax.fori_loop(0, slots // 32, fill, 0)

    pieces = []
    for b in range(bands):
        piece = arrived_ref[b * lanes : (b + 1) * lanes].astype(jnp.float32)
        pieces.append(piece.reshape(stacked, LANES).astype(jnp.bfloat16))
    by_part = jnp.dot(
        order_ref[...], jnp.concatenate(pieces, axis=1), preferred_element_type=jnp.float32
    ).astype(jnp.bfloat16)
    for member in range(2):
        columns = slice(member * half, (member + 1) * half)
        ordered[:, columns] = jnp.dot(
            by_part[member * stacked // 2 : (member + 1) * stacked // 2],
            hot[:, columns],
            preferred_element_type=jnp.float32,
        )

    def one_row(i, carry):
        n = scalars_ref[i]
        row = scalars_ref[rows + i]
        length = jnp.full((1, 1), n, jnp.int32).astype(jnp.float32)
        inverse = 1.0 / length
        norm = lax.rsqrt(length)
        kept = jnp.where(2 * wave < n, 1.0, 0.0)
        weight = kept * jnp.where(wave == 0, 1.0, 2.0)
        chosen = lax.broadcasted_iota(jnp.int32, (band_rows, 1), 0) == row
        row_factor[...] = jnp.sum(
            jnp.where(chosen, factor_ref[...].astype(jnp.float32), 0.0), axis=0, keepdims=True
        )
        for t in range(2):
            own = pl.ds(pl.multiple_of((t * rows + i) * fields, fields), fields)
            weighted = (ordered[own, :] * weight).astype(jnp.bfloat16)
            for b in range(high):
                part = weighted[:, b * LANES : (b + 1) * LANES]
                if t == 0:
                    lhs[b * fields : (b + 1) * fields, 0:LANES] = part
                    lhs[(high + b) * fields : (high + b + 1) * fields, LANES : 2 * LANES] = -part
                else:
                    lhs[b * fields : (b + 1) * fields, LANES : 2 * LANES] = part
                    lhs[(high + b) * fields : (high + b + 1) * fields, 0:LANES] = part

        low_wave = lax.broadcasted_iota(jnp.int32, (LANES, CHUNK), 0).astype(jnp.float32)
        place = lax.broadcasted_iota(jnp.int32, (LANES, CHUNK), 1).astype(jnp.float32)
        cos_state[...], sin_state[...] = cos_sin(low_wave * place, length, inverse)
        step_wave = lax.broadcasted_iota(jnp.int32, (LANES, LANES), 0).astype(jnp.float32)
        cos_step[...], sin_step[...] = cos_sin(step_wave * float(CHUNK), length, inverse)
        padded = cos_high.shape[0]
        high_wave = LANES * lax.broadcasted_iota(jnp.int32, (padded, CHUNK), 0)
        high_place = lax.broadcasted_iota(jnp.int32, (padded, CHUNK), 1)
        cos_high[...], sin_high[...] = cos_sin(
            (high_wave * high_place).astype(jnp.float32), length, inverse
        )
        cos_high_step[...], sin_high_step[...] = cos_sin(
            (high_wave * CHUNK).astype(jnp.float32), length, inverse
        )
        total[...] = jnp.zeros_like(total)
        grid_ref[i] = jnp.zeros(grid_ref.shape[1:], grid_ref.dtype)

        def chunk(h, carry):
            columns = pl.ds(pl.multiple_of(h * CHUNK, CHUNK), CHUNK)
            cosine, sine = cos_state[...], sin_state[...]
            table = jnp.concatenate([cosine, -sine], axis=0).astype(jnp.bfloat16)
            found = jnp.dot(lhs[...], table, preferred_element_type=jnp.float32)
            high_cos, high_sin = cos_high[...], sin_high[...]
            value = jnp.zeros((fields, CHUNK), jnp.float32)
            for b in range(high):
                real = found[b * fields : (b + 1) * fields]
                imag = found[(high + b) * fields : (high + b + 1) * fields]
                value = value + (real * high_cos[b : b + 1] - imag * high_sin[b : b + 1])
            at = h * CHUNK + lax.broadcasted_iota(jnp.int32, (1, CHUNK), 1)
            value = jnp.where(at < n, value * norm, 0.0).astype(jnp.bfloat16)
            grid_ref[i, :, columns] = value
            product = row_factor[:, columns] * value.astype(jnp.float32)
            product = product.astype(jnp.bfloat16).astype(jnp.float32)
            turned = [product * high_cos[b : b + 1] for b in range(high)]
            turned += [product * (-high_sin[b : b + 1]) for b in range(high)]
            turned = jnp.concatenate(turned, axis=0).astype(jnp.bfloat16)
            total[...] += lax.dot_general(
                turned, table, (((1,), (1,)), ((), ())), preferred_element_type=jnp.float32
            )
            step_cos = jnp.concatenate([cos_step[...]] * (CHUNK // LANES), axis=1)
            step_sin = jnp.concatenate([sin_step[...]] * (CHUNK // LANES), axis=1)
            cos_state[...] = cosine * step_cos - sine * step_sin
            sin_state[...] = sine * step_cos + cosine * step_sin
            high_step_cos, high_step_sin = cos_high_step[...], sin_high_step[...]
            cos_high[...] = high_cos * high_step_cos - high_sin * high_step_sin
            sin_high[...] = high_sin * high_step_cos + high_cos * high_step_sin
            return carry

        lax.fori_loop(0, (n + CHUNK - 1) // CHUNK, chunk, 0)

        scale = kept * norm
        for t in range(2):
            pieces = []
            for b in range(high):
                real = slice(b * fields, (b + 1) * fields)
                imag = slice((high + b) * fields, (high + b + 1) * fields)
                if t == 0:
                    pieces.append(total[real, 0:LANES] - total[imag, LANES : 2 * LANES])
                else:
                    pieces.append(total[imag, 0:LANES] + total[real, LANES : 2 * LANES])
            own = pl.ds(pl.multiple_of((t * rows + i) * fields, fields), fields)
            finished[own, :] = jnp.concatenate(pieces, axis=1) * scale
        return carry

    lax.fori_loop(0, rows, one_row, 0)

    pieces = []
    for member in range(2):
        columns = slice(member * half, (member + 1) * half)
        pieces.append(
            lax.dot_general(
                finished[:, columns].astype(jnp.bfloat16),
                hot[:, columns],
                (((1,), (1,)), ((), ())),
                preferred_element_type=jnp.float32,
            )
        )
    by_part = jnp.concatenate(pieces, axis=0).astype(jnp.bfloat16)
    by_lane = lax.dot_general(
        order_ref[...], by_part, (((0,), (0,)), ((), ())), preferred_element_type=jnp.float32
    )
    for b in range(bands):
        piece = by_lane[:, b * LANES : (b + 1) * LANES].reshape(lanes, stacked // lanes, LANES)
        out_ref[b * lanes : (b + 1) * lanes] = piece.astype(jnp.bfloat16)


def transform_rows(scalars, pair_band, arrived, factor, lanes, rows, fields, order):
    devices, chunk_rows, _ = arrived.shape
    band_rows, points = factor.shape
    pairs = pair_band.shape[0]
    waves = 2 * pairs
    high = waves // LANES
    padded = -(-high // 8) * 8
    stacked = 2 * high * fields
    wave_band = jnp.concatenate([pair_band, pair_band[::-1]])[None, :]
    return pl.pallas_call(
        functools.partial(row_kernel, lanes, band_rows),
        in_specs=[
            pl.BlockSpec(memory_space=pltpu.VMEM),
            pl.BlockSpec(memory_space=pltpu.SMEM),
            pl.BlockSpec(memory_space=pltpu.VMEM),
            pl.BlockSpec(memory_space=pltpu.VMEM),
            pl.BlockSpec(memory_space=pltpu.VMEM),
            pl.BlockSpec(memory_space=pltpu.VMEM),
        ],
        out_specs=[pl.BlockSpec(memory_space=pltpu.VMEM)] * 2,
        scratch_shapes=[
            pltpu.VMEM((devices // lanes * LANES, waves), jnp.bfloat16),
            pltpu.VMEM((2 * rows * fields, waves), jnp.float32),
            pltpu.VMEM((2 * rows * fields, waves), jnp.float32),
            pltpu.VMEM((stacked, 2 * LANES), jnp.bfloat16),
            pltpu.VMEM((stacked, 2 * LANES), jnp.float32),
            pltpu.VMEM((1, points), jnp.float32),
            pltpu.VMEM((LANES, CHUNK), jnp.float32),
            pltpu.VMEM((LANES, CHUNK), jnp.float32),
            pltpu.VMEM((LANES, LANES), jnp.float32),
            pltpu.VMEM((LANES, LANES), jnp.float32),
            pltpu.VMEM((padded, CHUNK), jnp.float32),
            pltpu.VMEM((padded, CHUNK), jnp.float32),
            pltpu.VMEM((padded, CHUNK), jnp.float32),
            pltpu.VMEM((padded, CHUNK), jnp.float32),
        ],
        out_shape=[
            jax.ShapeDtypeStruct((rows, fields, points), jnp.bfloat16),
            jax.ShapeDtypeStruct((devices, chunk_rows, LANES), jnp.bfloat16),
        ],
    )(order, scalars, wave_band, pair_band[:, None], arrived, factor)


def on_device(coefficients, cycle_length, row_latitude, pair_band, gridpoint_factor):
    bands, lanes = lax.axis_size("band"), lax.axis_size("lon")
    devices = bands * lanes
    lane = lax.axis_index("lon")
    device = lax.axis_index("band") * lanes + lane
    own_fields, slot_count, parts, latitudes = coefficients.shape
    band_rows, points = gridpoint_factor.shape
    fields = own_fields * lanes
    own_rows = -(-band_rows // lanes)
    lane_rows = np.arange(lanes * own_rows)
    inside = np.tile(lane_rows < band_rows, bands)
    clamped = np.minimum(lane_rows, band_rows - 1)
    row_ids = (np.arange(bands)[:, None] * band_rows + clamped[None, :]).reshape(-1)
    held = row_latitude if inside.all() else jnp.take(row_latitude, row_ids)
    onehot = held[:, None] == jnp.arange(latitudes, dtype=jnp.int32)[None, :]
    own = lax.dynamic_slice_in_dim(held, device * own_rows, own_rows)
    own_places = jnp.minimum(lane * own_rows + jnp.arange(own_rows), band_rows - 1)
    scalars = jnp.concatenate([jnp.take(cycle_length, own), own_places]).astype(jnp.int32)

    leaving = jnp.einsum(
        "rl,fstl->rtfs",
        onehot.astype(jnp.bfloat16),
        coefficients,
        preferred_element_type=jnp.float32,
    ).astype(jnp.bfloat16)
    leaving = jnp.pad(leaving, ((0, 0), (0, 0), (0, 0), (0, LANES - slot_count)))
    chunk_rows = own_rows * parts * own_fields
    leaving = leaving.reshape(devices, chunk_rows, LANES)
    arrived, factor = exchange(
        gather_kernel,
        bands,
        lanes,
        0,
        [
            jax.ShapeDtypeStruct((devices, chunk_rows, LANES), jnp.bfloat16),
            jax.ShapeDtypeStruct((band_rows, lanes * points), jnp.bfloat16),
        ],
        leaving,
        gridpoint_factor,
    )

    places = np.arange(lanes * chunk_rows).reshape(lanes, own_rows, parts, own_fields)
    places = places.transpose(2, 1, 0, 3).reshape(-1)
    order = jnp.asarray(
        places[:, None] == np.arange(lanes * chunk_rows)[None, :], dtype=jnp.bfloat16
    )
    grid, result = transform_rows(
        scalars, pair_band, arrived, factor, lanes, own_rows, fields, order
    )

    blocks, returned = exchange(
        scatter_kernel,
        bands,
        lanes,
        1,
        [
            jax.ShapeDtypeStruct((lanes, own_rows, fields, points), jnp.bfloat16),
            jax.ShapeDtypeStruct((devices, chunk_rows, LANES), jnp.bfloat16),
        ],
        grid,
        result,
    )
    grid_rows = blocks.reshape(lanes * own_rows, fields, points)[:band_rows]
    grid_rows = jnp.transpose(grid_rows, (1, 0, 2))
    returned = returned.reshape(devices * own_rows, parts, own_fields, LANES)
    back = onehot & inside[:, None]
    tendencies = jnp.einsum(
        "rtfs,rl->fstl",
        returned[..., :slot_count],
        back.astype(jnp.bfloat16),
        preferred_element_type=jnp.float32,
    ).astype(jnp.bfloat16)
    return (grid_rows, tendencies)


def solution(mesh):
    return jax.shard_map(
        on_device,
        mesh=mesh,
        in_specs=(P("lon", "band", None, None), P(), P(), P(), P("band", "lon")),
        out_specs=(P(None, "band", "lon"), P("lon", "band", None, None)),
        check_vma=False,
    )
```

time: 78.3 us -> 49.8 us (0.64); the launches traced: 77.1 us -> 50.4 us
  Pallas kernels: 9.31 us -> 41.7 us
  starting transfers between devices: 26.2 us -> 0 us
  local copies, waits for them, and re-layouts: 24.4 us -> 6.79 us
  waiting for transfers between devices: 12.7 us -> 0 us
  other arithmetic: 2.73 us -> 0.79 us
    pallas_call x1 -> x3, Pallas kernels: 9.31 us -> 41.7 us  [the longest x2 26.7 us: exchange(): pl.pallas_call(functools.partial(kernel, bands, lanes), out_shape=out_sha...]
    all_to_all x4 -> x0, starting transfers between devices: 26.2 us -> none  [the longest x1 10.3 us: on_device(): lax.all_to_all(grid, 'lon', split_axis=2, concat_axis=0, tiled=True)]
    all_to_all x4 -> x0, waiting for transfers between devices: 12.7 us -> none  [the longest x1 6.25 us: on_device(): lax.all_to_all(leaving, AXES, split_axis=0, concat_axis=0, tiled=True)]
    unnamed x9 -> x12, local copies, waits for them, and re-layouts: 7.78 us -> 2.15 us
    pallas_call x1 -> x0, local copies, waits for them, and re-layouts: 5.31 us -> none  [transform_rows(): pl.pallas_call(functools.partial(row_kernel, slot_count), grid_spec=grid_...]
    all_to_all x3 -> x0, local copies, waits for them, and re-layouts: 3.95 us -> none  [the longest x2 2.56 us: on_device(): lax.all_to_all(grid, 'lon', split_axis=2, concat_axis=0, tiled=True)]
    select_n x2, other arithmetic: 2.03 us -> 0.15 us  [on_device(): jnp.take(cycle_length, own)]
    pad x0 -> x1, local copies, waits for them, and re-layouts: none -> 0.8 us  [on_device(): jnp.pad(leaving, ((0, 0), (0, 0), (0, 0), (0, LANES - slot_count)))]
  transfers between devices with their start and end apart: 4 -> 0, of which waited for: 3 -> 0; matrix products, arithmetic and copies ran while one was open for 20% -> 0% of each run, Pallas kernels for 0% -> 0%
where the time goes in v2:
time: 49.8 us; the launch traced here: 50.4 us
  Pallas kernels  41.7 us (84%)
  local copies, waits for them, and re-layouts  6.79 us (14%)
  other arithmetic  0.79 us (2%)
  between operations  0.71 us (1%)
    pallas_call x2, Pallas kernels, exchange(): pl.pallas_call(functools.partial(kernel, bands, lanes), out_shape=out_sha...  26.7 us
    pallas_call x1, Pallas kernels, transform_rows(): pl.pallas_call(functools.partial(row_kernel, lanes, band_rows), in_specs=...  15 us
    unnamed x12, local copies, waits for them, and re-layouts  2.15 us
    reshape x1, local copies, waits for them, and re-layouts, on_device(): grid_rows = blocks.reshape(lanes * own_rows, fields, points)[:band_rows]  1.65 us

profile of v2, /device:TPU:0, one launch (start us, length us, event | category | flops | bytes accessed | tf_op | source)
XLA Modules:
  0.0 50.4 jit_solution(10323894286526946058)
XLA Ops:
  0.6 0.0 copy-start
  0.7 0.0 copy-start.4
  0.7 0.7 %copy-done.4 = s32[64]{0:T(128)S(1)} copy-done((s32[64]{0:T(128)S(1)}, s32[64]{0:T(128)}, u32[]{:S(2)}) %copy-start.4) | copy-done | bytes 280
  1.3 0.1 compare_select_fusion
  1.4 0.0 copy-start.1
  1.4 0.6 %copy-done.1 = s32[64]{0:T(128)S(1)} copy-done((s32[64]{0:T(128)S(1)}, s32[64]{0:T(128)}, u32[]{:S(2)}) %copy-start.1) | copy-done | bytes 280
  2.1 0.6 %gather_fusion = s32[2]{0:T(128)S(1)} fusion(s32[64]{0:T(128)S(1)} %copy-done.1, s32[1024]{0:T(1024)S(1)} %pad_clamp_fusion), kind=kCustom, calls=%fused_computation | custom fusion | bytes 24 | tf_op jit(solution)/shard_map/jit(_take)/gather | solution.py:388
  2.7 0.0 copy-start.3
  2.7 0.1 and_select_fusion
  2.8 0.6 %pad_add_fusion.1.scalars_ref = s32[4]{0:T(128)} fusion(s32[2]{0:T(128)S(1)} %get-tuple-element.19, s32[2]{0:T(128)S(1)} %get-tuple-element.18), kind=kLoop, calls=%fused_computation.15 | loop fusion | flops 4 | bytes 32 | tf_op jit(solution)/shard_map/concatenate | solution.py:388
  3.4 0.0 copy-done.3
  3.4 0.1 rev.3
  3.5 0.6 %broadcast_in_dim.13.wave_band_ref = s32[1,1280]{1,0:T(1,128)} reshape(s32[1280]{0:T(1024)S(1)} %pad_add_fusion) | data formatting | bytes 10240 | tf_op jit(solution)/shard_map/broadcast_in_dim | solution.py:336
  4.1 0.0 copy-done
  4.1 0.2 fusion
  4.4 0.1 copy.24
  4.5 0.8 %pad.4.clone = bf16[64,4,2,128]{3,2,1,0:T(2,128)(2,1)} pad(bf16[64,4,2,80]{3,2,1,0:T(2,128)(2,1)S(1)} %copy.24, bf16[]{:T(256)} %constant.38.clone.1), padding=0_0x0_0x0_0x0_48 | pad | bytes 212994 | tf_op jit(solution)/shard_map/jit(_pad)/pad | solution.py:396
  5.3 12.5 %shard_map.86 = (bf16[32,16,128]{2,1,0:T(8,128)(2,1)}, bf16[8,5632]{1,0:T(8,128)(2,1)}) custom-call(bf16[32,16,128]{2,1,0:T(8,128)(2,1)} %bitcast.19, bf16[8,1408]{1,0:T(8,128)(2,1)} %factor.1), custom_call_target="tpu_custom_call" | custom-call | tf_op jit(solution)/shard_map/pallas_call | solution.py:134
  17.8 0.9 %broadcast_in_dim.15.pair_band_ref = s32[640,1]{1,0:T(8,128)} reshape(s32[640]{0:T(1024)S(1)} %copy-done.3) | data formatting | bytes 5120 | tf_op jit(solution)/shard_map/broadcast_in_dim | solution.py:368
  18.7 15.0 %shard_map.87 = (bf16[2,8,5632]{2,1,0:T(8,128)(2,1)}, bf16[32,16,128]{2,1,0:T(8,128)(2,1)}) custom-call(bf16[64,64]{1,0:T(8,128)(2,1)} %constant.39.clone.order_ref, s32[4]{0:T(128)} %pad_add_fusion.1.scalars_ref, s32[1,1280]{1,0:T(1,128)} %broadcast_in_dim.13.wave_band_ref, s32[640,1]{1,0:T(8,128)} %broadcast_in_dim.15.pair_band_ref, ...), custom_call_target="tpu_custom_call" | custom-call | tf_op jit(solution)/shard_map/pallas_call | solution.py:337
  33.7 14.2 %shard_map.88 = (bf16[4,2,8,1408]{3,2,1,0:T(8,128)(2,1)}, bf16[32,16,128]{2,1,0:T(8,128)(2,1)}) custom-call(bf16[2,8,5632]{2,1,0:T(8,128)(2,1)} %get-tuple-element.10.grid, bf16[32,16,128]{2,1,0:T(8,128)(2,1)} %get-tuple-element.11.leaving), custom_call_target="tpu_custom_call" | custom-call | tf_op jit(solution)/shard_map/pallas_call | solution.py:134
  47.9 0.0 copy-start.2
  47.9 1.6 %copy.28 = bf16[8,8,1408]{2,0,1:T(8,128)(2,1)} copy(bf16[8,8,1408]{2,1,0:T(8,128)(2,1)} %bitcast.21) | data formatting | bytes 360448 | tf_op jit(solution)/shard_map/reshape | solution.py:433
  49.6 0.0 copy-done.2
  49.6 0.2 fusion.1
  49.7 0.7 %copy.19 = bf16[2,80,4,64]{1,3,2,0:T(8,128)(2,1)} copy(bf16[2,80,4,64]{1,3,0,2:T(8,128)(2,1)S(1)} %fusion.1) | data formatting | bytes 163840
  (2 shorter events, 0.0 us)
Async XLA Ops:
  0.6 3.5 %copy-start = (bf16[2,80,4,64]{1,3,2,0:T(8,128)(2,1)S(1)}, bf16[2,80,4,64]{1,3,2,0:T(8,128)(2,1)}, u32[]{:S(2)}) copy-start(bf16[2,80,4,64]{1,3,2,0:T(8,128)(2,1)} %param.7) | copy-start | bytes 245764
  0.7 0.7 %copy-start.4 = (s32[64]{0:T(128)S(1)}, s32[64]{0:T(128)}, u32[]{:S(2)}) copy-start(s32[64]{0:T(128)} %param.9) | copy-start | bytes 772
  1.4 0.7 %copy-start.1 = (s32[64]{0:T(128)S(1)}, s32[64]{0:T(128)}, u32[]{:S(2)}) copy-start(s32[64]{0:T(128)} %param.8) | copy-start | bytes 772
  2.7 0.7 %copy-start.3 = (s32[640]{0:T(1024)S(1)}, s32[640]{0:T(1024)}, u32[]{:S(2)}) copy-start(s32[640]{0:T(1024)} %param.10) | copy-start | bytes 7684
  47.9 1.7 %copy-start.2 = (bf16[32,16,128]{2,1,0:T(8,128)(2,1)S(1)}, bf16[32,16,128]{2,1,0:T(8,128)(2,1)}, u32[]{:S(2)}) copy-start(bf16[32,16,128]{2,1,0:T(8,128)(2,1)} %get-tuple-element.13) | copy-start | bytes 393220

commit v3 on v2

v3 whole, which is shorter than its diff:
```python
import functools
import math

import jax
import jax.numpy as jnp
import numpy as np
from jax import lax
from jax.experimental import pallas as pl
from jax.experimental.pallas import tpu as pltpu
from jax.sharding import PartitionSpec as P

TWO_PI = 2.0 * math.pi
LANES = 128
CHUNK = 256


def cos_sin(product, length, inverse):
    turns = jnp.floor(product * inverse + 0.5)
    half = (product - turns * length) * (inverse * (0.5 * TWO_PI))
    square = half * half
    sine = jnp.full_like(half, -1.0 / math.factorial(11))
    for order in (9, 7, 5, 3, 1):
        sine = sine * square + (-1.0) ** (order // 2) / math.factorial(order)
    sine = sine * half
    cosine = jnp.full_like(half, 1.0 / math.factorial(12))
    for order in (10, 8, 6, 4, 2, 0):
        cosine = cosine * square + (-1.0) ** (order // 2) / math.factorial(order)
    return 1.0 - 2.0 * sine * sine, 2.0 * sine * cosine


MESH = pl.DeviceIdType.MESH


def round_kernel(
    bands,
    lanes,
    slot_count,
    cycle_ref,
    latitude_ref,
    order_ref,
    pair_band_ref,
    leaving,
    factor_ref,
    blocks,
    returned,
    arrived,
    cycles,
    grid_ref,
    result,
    hot,
    ordered,
    finished,
    lhs,
    total,
    row_factor,
    cos_state,
    sin_state,
    cos_step,
    sin_step,
    cos_high,
    sin_high,
    cos_high_step,
    sin_high_step,
    send_sem,
    recv_sem,
    back_send_sem,
    back_recv_sem,
    factor_send_sem,
    factor_recv_sem,
    grid_send_sem,
    grid_recv_sem,
):
    band, lane = lax.axis_index("band"), lax.axis_index("lon")
    me = band * lanes + lane
    devices = bands * lanes
    band_rows, points = factor_ref.shape
    rows, fields = grid_ref.shape[0], grid_ref.shape[1]
    slots, waves = hot.shape
    high = waves // LANES
    half = waves // 2
    stacked = leaving.shape[1] * lanes

    def peer(k):
        flat = lax.rem(me + k, devices)
        return flat, {"band": flat // lanes, "lon": lax.rem(flat, lanes)}

    def block_of(index):
        return pl.ds(pl.multiple_of(index * points, LANES), points)

    def send_chunks(source, target, sent, received):
        def send(k, carry):
            flat, device = peer(k)
            pltpu.make_async_remote_copy(
                src_ref=source.at[flat],
                dst_ref=target.at[me],
                send_sem=sent,
                recv_sem=received,
                device_id=device,
                device_id_type=MESH,
            ).start()
            return carry

        lax.fori_loop(1, devices, send, 0)
        target[me] = source[me]

    def wait_chunks(source, target, sent, received):
        pltpu.make_async_remote_copy(
            src_ref=source.at[pl.ds(0, devices - 1)],
            dst_ref=target.at[pl.ds(0, devices - 1)],
            send_sem=sent,
            recv_sem=received,
            device_id={"band": band, "lon": lane},
            device_id_type=MESH,
        ).wait()

    def factor_copy(j):
        return pltpu.make_async_remote_copy(
            src_ref=factor_ref,
            dst_ref=cycles.at[:, block_of(lane)],
            send_sem=factor_send_sem.at[j],
            recv_sem=factor_recv_sem.at[j],
            device_id={"lon": lax.rem(lane + j, lanes)},
            device_id_type=MESH,
        )

    def grid_copy(i, j):
        other = lax.rem(lane + j, lanes)
        return pltpu.make_async_remote_copy(
            src_ref=grid_ref.at[i, :, block_of(other)],
            dst_ref=blocks.at[lane, i],
            send_sem=grid_send_sem.at[i, j],
            recv_sem=grid_recv_sem.at[i, j],
            device_id={"lon": other},
            device_id_type=MESH,
        )

    barrier = pltpu.get_barrier_semaphore()

    def signal(k, carry):
        pl.semaphore_signal(barrier, inc=1, device_id=peer(k)[1], device_id_type=MESH)
        return carry

    lax.fori_loop(1, devices, signal, 0)

    pair_band = pair_band_ref[...]
    source = lax.broadcasted_iota(jnp.int32, (half, half), 0)
    target = lax.broadcasted_iota(jnp.int32, (half, half), 1)
    earlier = jnp.where(source < target, 1.0, 0.0).astype(jnp.bfloat16)
    mirror = jnp.where(source == half - 1 - target, 1.0, 0.0).astype(jnp.bfloat16)
    padded_bands = -(-bands // 8) * 8
    owner = lax.broadcasted_iota(jnp.int32, (padded_bands, half), 0) == pair_band
    counts = jnp.dot(
        jnp.where(owner, 1.0, 0.0).astype(jnp.bfloat16), earlier, preferred_element_type=jnp.float32
    )
    place = jnp.sum(jnp.where(owner, counts, 0.0), axis=0, keepdims=True)
    pair = jnp.concatenate([pair_band.astype(jnp.float32)] * 4 + [place] * 4, axis=0)
    flipped = jnp.dot(pair.astype(jnp.bfloat16), mirror, preferred_element_type=jnp.float32)
    both = jnp.concatenate([pair, flipped], axis=1)
    slot_of_wave = (both[0:1] * LANES + both[4:5]).astype(jnp.int32)

    def fill(step, carry):
        start = pl.multiple_of(step * 32, 32)
        slot = lax.broadcasted_iota(jnp.int32, (32, waves), 0) + start
        hot[pl.ds(start, 32), :] = jnp.where(slot == slot_of_wave, 1.0, 0.0).astype(jnp.bfloat16)
        return carry

    lax.fori_loop(0, slots // 32, fill, 0)

    pl.semaphore_wait(barrier, devices - 1)
    send_chunks(leaving, arrived, send_sem, recv_sem)
    for j in range(1, lanes):
        factor_copy(j).start()
    cycles[:, block_of(lane)] = factor_ref[...]

    wave = lax.broadcasted_iota(jnp.int32, (1, waves), 1)

    def length_of(i):
        row = jnp.minimum(lane * rows + i, band_rows - 1)
        n = cycle_ref[latitude_ref[band * band_rows + row]]
        length = jnp.full((1, 1), n, jnp.int32).astype(jnp.float32)
        return row, n, length, 1.0 / length

    def prepare(i, carry):
        row, n, length, inverse = length_of(i)
        low_wave = lax.broadcasted_iota(jnp.int32, (LANES, CHUNK), 0).astype(jnp.float32)
        place = lax.broadcasted_iota(jnp.int32, (LANES, CHUNK), 1).astype(jnp.float32)
        cos_state[i], sin_state[i] = cos_sin(low_wave * place, length, inverse)
        step_wave = lax.broadcasted_iota(jnp.int32, (LANES, LANES), 0).astype(jnp.float32)
        cos_step[i], sin_step[i] = cos_sin(step_wave * float(CHUNK), length, inverse)
        padded = cos_high.shape[1]
        high_wave = LANES * lax.broadcasted_iota(jnp.int32, (padded, CHUNK), 0)
        high_place = lax.broadcasted_iota(jnp.int32, (padded, CHUNK), 1)
        cos_high[i], sin_high[i] = cos_sin(
            (high_wave * high_place).astype(jnp.float32), length, inverse
        )
        cos_high_step[i], sin_high_step[i] = cos_sin(
            (high_wave * CHUNK).astype(jnp.float32), length, inverse
        )
        return carry

    lax.fori_loop(0, rows, prepare, 0)

    for j in range(1, lanes):
        factor_copy(j).wait()
    wait_chunks(leaving, arrived, send_sem, recv_sem)

    pieces = []
    for b in range(bands):
        piece = arrived[b * lanes : (b + 1) * lanes].astype(jnp.float32)
        pieces.append(piece.reshape(stacked, LANES).astype(jnp.bfloat16))
    by_part = jnp.dot(
        order_ref[...], jnp.concatenate(pieces, axis=1), preferred_element_type=jnp.float32
    ).astype(jnp.bfloat16)
    for member in range(2):
        columns = slice(member * half, (member + 1) * half)
        ordered[:, columns] = jnp.dot(
            by_part[member * stacked // 2 : (member + 1) * stacked // 2],
            hot[:, columns],
            preferred_element_type=jnp.float32,
        )

    def one_row(i, carry):
        row, n, length, inverse = length_of(i)
        norm = lax.rsqrt(length)
        kept = jnp.where(2 * wave < n, 1.0, 0.0)
        weight = kept * jnp.where(wave == 0, 1.0, 2.0)
        chosen = lax.broadcasted_iota(jnp.int32, (band_rows, 1), 0) == row
        row_factor[...] = jnp.sum(
            jnp.where(chosen, cycles[...].astype(jnp.float32), 0.0), axis=0, keepdims=True
        )
        for t in range(2):
            own = pl.ds(pl.multiple_of((t * rows + i) * fields, fields), fields)
            weighted = (ordered[own, :] * weight).astype(jnp.bfloat16)
            for b in range(high):
                part = weighted[:, b * LANES : (b + 1) * LANES]
                if t == 0:
                    lhs[b * fields : (b + 1) * fields, 0:LANES] = part
                    lhs[(high + b) * fields : (high + b + 1) * fields, LANES : 2 * LANES] = -part
                else:
                    lhs[b * fields : (b + 1) * fields, LANES : 2 * LANES] = part
                    lhs[(high + b) * fields : (high + b + 1) * fields, 0:LANES] = part

        total[...] = jnp.zeros_like(total)

        def chunk(h, carry):
            columns = pl.ds(pl.multiple_of(h * CHUNK, CHUNK), CHUNK)
            cosine, sine = cos_state[i], sin_state[i]
            table = jnp.concatenate([cosine, -sine], axis=0).astype(jnp.bfloat16)
            found = jnp.dot(lhs[...], table, preferred_element_type=jnp.float32)
            high_cos, high_sin = cos_high[i], sin_high[i]
            value = jnp.zeros((fields, CHUNK), jnp.float32)
            for b in range(high):
                real = found[b * fields : (b + 1) * fields]
                imag = found[(high + b) * fields : (high + b + 1) * fields]
                value = value + (real * high_cos[b : b + 1] - imag * high_sin[b : b + 1])
            at = h * CHUNK + lax.broadcasted_iota(jnp.int32, (1, CHUNK), 1)
            value = jnp.where(at < n, value * norm, 0.0).astype(jnp.bfloat16)
            grid_ref[i, :, columns] = value
            product = row_factor[:, columns] * value.astype(jnp.float32)
            product = product.astype(jnp.bfloat16).astype(jnp.float32)
            turned = [product * high_cos[b : b + 1] for b in range(high)]
            turned += [product * (-high_sin[b : b + 1]) for b in range(high)]
            turned = jnp.concatenate(turned, axis=0).astype(jnp.bfloat16)
            total[...] += lax.dot_general(
                turned, table, (((1,), (1,)), ((), ())), preferred_element_type=jnp.float32
            )
            step_cos = jnp.concatenate([cos_step[i]] * (CHUNK // LANES), axis=1)
            step_sin = jnp.concatenate([sin_step[i]] * (CHUNK // LANES), axis=1)
            cos_state[i] = cosine * step_cos - sine * step_sin
            sin_state[i] = sine * step_cos + cosine * step_sin
            high_step_cos, high_step_sin = cos_high_step[i], sin_high_step[i]
            cos_high[i] = high_cos * high_step_cos - high_sin * high_step_sin
            sin_high[i] = high_sin * high_step_cos + high_cos * high_step_sin
            return carry

        lax.fori_loop(0, lanes * points // CHUNK, chunk, 0)

        for j in range(1, lanes):
            grid_copy(i, j).start()
        blocks[lane, i] = grid_ref[i, :, block_of(lane)]

        scale = kept * norm
        for t in range(2):
            pieces = []
            for b in range(high):
                real = slice(b * fields, (b + 1) * fields)
                imag = slice((high + b) * fields, (high + b + 1) * fields)
                if t == 0:
                    pieces.append(total[real, 0:LANES] - total[imag, LANES : 2 * LANES])
                else:
                    pieces.append(total[imag, 0:LANES] + total[real, LANES : 2 * LANES])
            own = pl.ds(pl.multiple_of((t * rows + i) * fields, fields), fields)
            finished[own, :] = jnp.concatenate(pieces, axis=1) * scale
        return carry

    lax.fori_loop(0, rows, one_row, 0)
    pieces = []
    for member in range(2):
        columns = slice(member * half, (member + 1) * half)
        pieces.append(
            lax.dot_general(
                finished[:, columns].astype(jnp.bfloat16),
                hot[:, columns],
                (((1,), (1,)), ((), ())),
                preferred_element_type=jnp.float32,
            )
        )
    by_part = jnp.concatenate(pieces, axis=0).astype(jnp.bfloat16)
    by_lane = lax.dot_general(
        order_ref[...], by_part, (((0,), (0,)), ((), ())), preferred_element_type=jnp.float32
    )
    for b in range(bands):
        piece = by_lane[:, b * LANES : (b + 1) * LANES].reshape(lanes, stacked // lanes, LANES)
        result[b * lanes : (b + 1) * lanes] = piece.astype(jnp.bfloat16)

    send_chunks(result, returned, back_send_sem, back_recv_sem)
    for i in range(rows):
        for j in range(1, lanes):
            grid_copy(i, j).wait()
    wait_chunks(result, returned, back_send_sem, back_recv_sem)


def round_trip(cycle_length, held, order, pair_band, leaving, factor, bands, lanes, fields, slot_count):
    devices, chunk_rows, _ = leaving.shape
    band_rows, points = factor.shape
    waves = 2 * pair_band.shape[0]
    rows = -(-band_rows // lanes)
    high = waves // LANES
    padded = -(-high // 8) * 8
    stacked = 2 * high * fields
    chunks = (devices, chunk_rows, LANES)
    return pl.pallas_call(
        functools.partial(round_kernel, bands, lanes, slot_count),
        in_specs=[pl.BlockSpec(memory_space=pltpu.SMEM)] * 2
        + [pl.BlockSpec(memory_space=pltpu.VMEM)] * 4,
        out_specs=[pl.BlockSpec(memory_space=pltpu.VMEM)] * 2,
        scratch_shapes=[
            pltpu.VMEM(chunks, jnp.bfloat16),
            pltpu.VMEM((band_rows, lanes * points), jnp.bfloat16),
            pltpu.VMEM((rows, fields, lanes * points), jnp.bfloat16),
            pltpu.VMEM(chunks, jnp.bfloat16),
            pltpu.VMEM((bands * LANES, waves), jnp.bfloat16),
            pltpu.VMEM((2 * rows * fields, waves), jnp.float32),
            pltpu.VMEM((2 * rows * fields, waves), jnp.float32),
            pltpu.VMEM((stacked, 2 * LANES), jnp.bfloat16),
            pltpu.VMEM((stacked, 2 * LANES), jnp.float32),
            pltpu.VMEM((1, lanes * points), jnp.float32),
            pltpu.VMEM((rows, LANES, CHUNK), jnp.float32),
            pltpu.VMEM((rows, LANES, CHUNK), jnp.float32),
            pltpu.VMEM((rows, LANES, LANES), jnp.float32),
            pltpu.VMEM((rows, LANES, LANES), jnp.float32),
            pltpu.VMEM((rows, padded, CHUNK), jnp.float32),
            pltpu.VMEM((rows, padded, CHUNK), jnp.float32),
            pltpu.VMEM((rows, padded, CHUNK), jnp.float32),
            pltpu.VMEM((rows, padded, CHUNK), jnp.float32),
        ]
        + [pltpu.SemaphoreType.DMA] * 4
        + [pltpu.SemaphoreType.DMA((lanes,))] * 2
        + [pltpu.SemaphoreType.DMA((rows, lanes))] * 2,
        out_shape=[
            jax.ShapeDtypeStruct((lanes, rows, fields, points), jnp.bfloat16),
            jax.ShapeDtypeStruct(chunks, jnp.bfloat16),
        ],
        compiler_params=pltpu.CompilerParams(collective_id=0, has_side_effects=True),
    )(cycle_length, held, order, pair_band[None, :], leaving, factor)


def on_device(coefficients, cycle_length, row_latitude, pair_band, gridpoint_factor):
    bands, lanes = lax.axis_size("band"), lax.axis_size("lon")
    devices = bands * lanes
    own_fields, slot_count, parts, latitudes = coefficients.shape
    band_rows, points = gridpoint_factor.shape
    fields = own_fields * lanes
    own_rows = -(-band_rows // lanes)
    lane_rows = np.arange(lanes * own_rows)
    inside = np.tile(lane_rows < band_rows, bands)
    clamped = np.minimum(lane_rows, band_rows - 1)
    row_ids = (np.arange(bands)[:, None] * band_rows + clamped[None, :]).reshape(-1)
    held = row_latitude if inside.all() else jnp.take(row_latitude, row_ids)
    onehot = held[:, None] == jnp.arange(latitudes, dtype=jnp.int32)[None, :]
    leaving = jnp.einsum(
        "rl,fstl->rtfs",
        onehot.astype(jnp.bfloat16),
        coefficients,
        preferred_element_type=jnp.float32,
    ).astype(jnp.bfloat16)
    leaving = jnp.pad(leaving, ((0, 0), (0, 0), (0, 0), (0, LANES - slot_count)))
    chunk_rows = own_rows * parts * own_fields
    leaving = leaving.reshape(devices, chunk_rows, LANES)
    places = np.arange(lanes * chunk_rows).reshape(lanes, own_rows, parts, own_fields)
    places = places.transpose(2, 1, 0, 3).reshape(-1)
    order = jnp.asarray(
        places[:, None] == np.arange(lanes * chunk_rows)[None, :], dtype=jnp.bfloat16
    )
    blocks, returned = round_trip(
        cycle_length,
        row_latitude,
        order,
        pair_band,
        leaving,
        gridpoint_factor,
        bands,
        lanes,
        fields,
        slot_count,
    )
    grid_rows = blocks.reshape(lanes * own_rows, fields, points)[:band_rows]
    grid_rows = jnp.transpose(grid_rows, (1, 0, 2))
    returned = returned.reshape(devices * own_rows, parts, own_fields, LANES)
    back = onehot & inside[:, None]
    tendencies = jnp.einsum(
        "rtfs,rl->fstl",
        returned[..., :slot_count],
        back.astype(jnp.bfloat16),
        preferred_element_type=jnp.float32,
    ).astype(jnp.bfloat16)
    return (grid_rows, tendencies)


def solution(mesh):
    return jax.shard_map(
        on_device,
        mesh=mesh,
        in_specs=(P("lon", "band", None, None), P(), P(), P(), P("band", "lon")),
        out_specs=(P(None, "band", "lon"), P("lon", "band", None, None)),
        check_vma=False,
    )
```

time: 49.8 us -> 44.2 us (0.89); the launches traced: 50.4 us -> 44 us
  Pallas kernels: 41.7 us -> 37.7 us
  local copies, waits for them, and re-layouts: 6.79 us -> 5.22 us
  other arithmetic: 0.79 us -> 0 us
    pallas_call x3 -> x1, Pallas kernels: 41.7 us -> 37.7 us  [round_trip(): pl.pallas_call(functools.partial(round_kernel, bands, lanes, slot_count),...]
    unnamed x12 -> x10, local copies, waits for them, and re-layouts: 2.15 us -> 1.47 us
    gather x1 -> x0, local copies, waits for them, and re-layouts: 0.64 us -> none  [on_device(): jnp.take(cycle_length, own)]
    concatenate x2 -> x0, other arithmetic: 0.63 us -> none  [the longest x1 0.62 us: on_device(): jnp.concatenate([jnp.take(cycle_length, own), own_places]).astype(jnp.int32)]
    broadcast_in_dim x2 -> x1, local copies, waits for them, and re-layouts: 1.47 us -> 1.3 us  [round_trip(): pair_band[None, :]]
where the time goes in v3:
time: 44.2 us; the launch traced here: 44 us
  Pallas kernels  37.7 us (85%)
  local copies, waits for them, and re-layouts  5.22 us (12%)
  between operations  0.69 us (2%)
    pallas_call x1, Pallas kernels, round_trip(): pl.pallas_call(functools.partial(round_kernel, bands, lanes, slot_count),...  37.7 us
    reshape x1, local copies, waits for them, and re-layouts, on_device(): grid_rows = blocks.reshape(lanes * own_rows, fields, points)[:band_rows]  1.65 us
    unnamed x10, local copies, waits for them, and re-layouts  1.47 us
    broadcast_in_dim x1, local copies, waits for them, and re-layouts, round_trip(): pair_band[None, :]  1.3 us

profile of v3, /device:TPU:0, one launch (start us, length us, event | category | flops | bytes accessed | tf_op | source)
XLA Modules:
  0.0 44.0 jit_solution(16837335886426281034)
XLA Ops:
  0.6 0.0 copy-start
  0.6 0.0 copy-start.2
  0.7 1.3 %broadcast_in_dim.2.pair_band_ref = s32[1,640]{1,0:T(1,128)} reshape(s32[640]{0:T(1024)} %param.10) | data formatting | bytes 5120 | tf_op jit(solution)/shard_map/broadcast_in_dim | solution.py:365
  2.0 0.0 copy-done
  2.0 0.0 copy-done.2
  2.0 0.2 fusion
  2.2 0.1 copy.18
  2.3 0.8 %pad.4.clone = bf16[64,4,2,128]{3,2,1,0:T(2,128)(2,1)} pad(bf16[64,4,2,80]{3,2,1,0:T(2,128)(2,1)S(1)} %copy.18, bf16[]{:T(256)} %constant.6.clone.1), padding=0_0x0_0x0_0x0_48 | pad | bytes 212994 | tf_op jit(solution)/shard_map/jit(_pad)/pad | solution.py:387
  3.1 37.7 %shard_map.86 = (bf16[4,2,8,1408]{3,2,1,0:T(8,128)(2,1)}, bf16[32,16,128]{2,1,0:T(8,128)(2,1)}) custom-call(s32[64]{0:T(128)} %cycle_ref.1, s32[64]{0:T(128)} %latitude_ref.1, bf16[64,64]{1,0:T(8,128)(2,1)} %constant.7.clone.order_ref, s32[1,640]{1,0:T(1,128)} %broadcast_in_dim.2.pair_band_ref, bf16[32,16,128]{2,1,0:T(8,128)(2,1)} %bitcast.19, ...), custom_call_target="tpu_custom_call" | custom-call | tf_op jit(solution)/shard_map/pallas_call | solution.py:332
  40.8 0.0 copy-start.1
  40.8 1.6 %copy.22 = bf16[8,8,1408]{2,0,1:T(8,128)(2,1)} copy(bf16[8,8,1408]{2,1,0:T(8,128)(2,1)} %bitcast.21) | data formatting | bytes 360448 | tf_op jit(solution)/shard_map/reshape | solution.py:407
  42.5 0.0 copy-start.3
  42.5 0.0 copy-done.1
  42.5 0.7 %copy-done.3 = s32[64]{0:T(128)S(1)} copy-done((s32[64]{0:T(128)S(1)}, s32[64]{0:T(128)}, u32[]{:S(2)}) %copy-start.3) | copy-done | bytes 280
  43.1 0.2 fusion.1
  43.3 0.7 %copy.13 = bf16[2,80,4,64]{1,3,2,0:T(8,128)(2,1)} copy(bf16[2,80,4,64]{1,3,0,2:T(8,128)(2,1)S(1)} %fusion.1) | data formatting | bytes 163840
Async XLA Ops:
  0.6 1.3 %copy-start = (bf16[2,80,4,64]{1,3,2,0:T(8,128)(2,1)S(1)}, bf16[2,80,4,64]{1,3,2,0:T(8,128)(2,1)}, u32[]{:S(2)}) copy-start(bf16[2,80,4,64]{1,3,2,0:T(8,128)(2,1)} %param.7) | copy-start | bytes 245764
  0.6 1.3 %copy-start.2 = (s32[64]{0:T(128)S(1)}, s32[64]{0:T(128)}, u32[]{:S(2)}) copy-start(s32[64]{0:T(128)} %latitude_ref.1) | copy-start | bytes 772
  40.8 1.7 %copy-start.1 = (bf16[32,16,128]{2,1,0:T(8,128)(2,1)S(1)}, bf16[32,16,128]{2,1,0:T(8,128)(2,1)}, u32[]{:S(2)}) copy-start(bf16[32,16,128]{2,1,0:T(8,128)(2,1)} %get-tuple-element.5) | copy-start | bytes 393220
  42.5 0.7 %copy-start.3 = (s32[64]{0:T(128)S(1)}, s32[64]{0:T(128)}, u32[]{:S(2)}) copy-start(s32[64]{0:T(128)} %latitude_ref.1) | copy-start | bytes 772

commit v4 on v3

--- a/solution.py
+++ b/solution.py
@@ -34,7 +34,6 @@
 def round_kernel(
     bands,
     lanes,
-    slot_count,
     cycle_ref,
     latitude_ref,
     order_ref,
@@ -142,7 +141,7 @@
 
     lax.fori_loop(1, devices, signal, 0)
 
-    pair_band = pair_band_ref[...]
+    pair_band = pair_band_ref[...].reshape(1, half)
     source = lax.broadcasted_iota(jnp.int32, (half, half), 0)
     target = lax.broadcasted_iota(jnp.int32, (half, half), 1)
     earlier = jnp.where(source < target, 1.0, 0.0).astype(jnp.bfloat16)
@@ -200,8 +199,6 @@
 
     lax.fori_loop(0, rows, prepare, 0)
 
-    for j in range(1, lanes):
-        factor_copy(j).wait()
     wait_chunks(leaving, arrived, send_sem, recv_sem)
 
     pieces = []
@@ -218,6 +215,9 @@
             hot[:, columns],
             preferred_element_type=jnp.float32,
         )
+
+    for j in range(1, lanes):
+        factor_copy(j).wait()
 
     def one_row(i, carry):
         row, n, length, inverse = length_of(i)
@@ -273,7 +273,7 @@
             sin_high[i] = high_sin * high_step_cos + high_cos * high_step_sin
             return carry
 
-        lax.fori_loop(0, lanes * points // CHUNK, chunk, 0)
+        lax.fori_loop(0, lanes * points // CHUNK, chunk, 0, unroll=True)
 
         for j in range(1, lanes):
             grid_copy(i, j).start()
@@ -320,7 +320,7 @@
     wait_chunks(result, returned, back_send_sem, back_recv_sem)
 
 
-def round_trip(cycle_length, held, order, pair_band, leaving, factor, bands, lanes, fields, slot_count):
+def round_trip(cycle_length, held, order, pair_band, leaving, factor, bands, lanes, fields):
     devices, chunk_rows, _ = leaving.shape
     band_rows, points = factor.shape
     waves = 2 * pair_band.shape[0]
@@ -330,7 +330,7 @@
     stacked = 2 * high * fields
     chunks = (devices, chunk_rows, LANES)
     return pl.pallas_call(
-        functools.partial(round_kernel, bands, lanes, slot_count),
+        functools.partial(round_kernel, bands, lanes),
         in_specs=[pl.BlockSpec(memory_space=pltpu.SMEM)] * 2
         + [pl.BlockSpec(memory_space=pltpu.VMEM)] * 4,
         out_specs=[pl.BlockSpec(memory_space=pltpu.VMEM)] * 2,
@@ -361,8 +361,12 @@
             jax.ShapeDtypeStruct((lanes, rows, fields, points), jnp.bfloat16),
             jax.ShapeDtypeStruct(chunks, jnp.bfloat16),
         ],
-        compiler_params=pltpu.CompilerParams(collective_id=0, has_side_effects=True),
-    )(cycle_length, held, order, pair_band[None, :], leaving, factor)
+        compiler_params=pltpu.CompilerParams(
+            collective_id=0,
+            has_side_effects=True,
+            vmem_limit_bytes=(12 << 20) + 4 * bands * LANES * waves,
+        ),
+    )(cycle_length, held, order, pair_band, leaving, factor)
 
 
 def on_device(coefficients, cycle_length, row_latitude, pair_band, gridpoint_factor):
@@ -402,7 +406,6 @@
         bands,
         lanes,
         fields,
-        slot_count,
     )
     grid_rows = blocks.reshape(lanes * own_rows, fields, points)[:band_rows]
     grid_rows = jnp.transpose(grid_rows, (1, 0, 2))

time: 44.2 us -> 30.5 us (0.69)
  Pallas kernels: 37.7 us -> 25.3 us
  local copies, waits for them, and re-layouts: 5.22 us -> 3.21 us
  matrix products: 0.39 us -> 1.04 us
    pallas_call x1, Pallas kernels: 37.7 us -> 25.3 us  [round_trip(): pl.pallas_call(functools.partial(round_kernel, bands, lanes), in_specs=[p...]
    broadcast_in_dim x1 -> x0, local copies, waits for them, and re-layouts: 1.3 us -> none  [round_trip(): pair_band[None, :]]
    reshape x1, local copies, waits for them, and re-layouts: 1.65 us -> 0.69 us  [on_device(): grid_rows = blocks.reshape(lanes * own_rows, fields, points)[:band_rows]]
    unnamed x10 -> x14, local copies, waits for them, and re-layouts: 1.47 us -> 2.38 us
    pad x1, local copies, waits for them, and re-layouts: 0.8 us -> 0.14 us  [on_device(): jnp.pad(leaving, ((0, 0), (0, 0), (0, 0), (0, LANES - slot_count)))]
    dot_general x1, matrix products: 0.23 us -> 0.88 us  [on_device(): jnp.einsum('rl,fstl->rtfs', onehot.astype(jnp.bfloat16), coefficients, pr...]
where the time goes in v4:
time: 30.5 us; the launch traced here: 30.3 us
  Pallas kernels  25.3 us (83%)
  local copies, waits for them, and re-layouts  3.21 us (11%)
  matrix products  1.04 us (3%)
  between operations  0.72 us (2%)
    pallas_call x1, Pallas kernels, round_trip(): pl.pallas_call(functools.partial(round_kernel, bands, lanes), in_specs=[p...  25.3 us
    unnamed x14, local copies, waits for them, and re-layouts  2.38 us
    dot_general x1, matrix products, on_device(): jnp.einsum('rl,fstl->rtfs', onehot.astype(jnp.bfloat16), coefficients, pr...  0.88 us
    reshape x1, local copies, waits for them, and re-layouts, on_device(): grid_rows = blocks.reshape(lanes * own_rows, fields, points)[:band_rows]  0.69 us

profile of v4, /device:TPU:0, one launch (start us, length us, event | category | flops | bytes accessed | tf_op | source)
XLA Modules:
  0.0 30.3 jit_solution(337906736845419820)
XLA Ops:
  0.6 0.0 copy-start
  0.6 0.9 %copy-done = bf16[2,80,4,64]{1,3,2,0:T(8,128)(2,1)S(1)} copy-done((bf16[2,80,4,64]{1,3,2,0:T(8,128)(2,1)S(1)}, bf16[2,80,4,64]{1,3,2,0:T(8,128)(2,1)}, u32[]{:S(2)}) %copy-start) | copy-done | bytes 81944
  1.5 0.9 %fusion = bf16[64,4,2,80]{3,0,1,2:T(8,128)(2,1)S(1)} fusion(bf16[2,80,4,64]{1,3,2,0:T(8,128)(2,1)S(1)} %copy-done, s32[64]{0:T(128)} %latitude_ref.1), kind=kOutput, calls=%fused_computation.2 | convolution fusion | flops 5287936 | bytes 164096 | tf_op jit(solution)/shard_map/rl,fstl->rtfs/dot_general | solution.py:385
  2.4 0.1 copy.18
  2.6 0.0 copy-start.1
  2.6 0.0 copy-start.2
  2.6 0.0 copy-start.4
  2.6 0.1 pad.4.clone
  2.8 0.0 copy-start.3
  2.8 0.0 copy-start.5
  2.8 0.5 %copy-done.1 = bf16[8,1408]{1,0:T(8,128)(2,1)S(1)} copy-done((bf16[8,1408]{1,0:T(8,128)(2,1)S(1)}, bf16[8,1408]{1,0:T(8,128)(2,1)}, u32[]{:S(2)}) %copy-start.1) | copy-done | bytes 22552
  3.3 0.0 copy-done.2
  3.3 0.0 copy-done.4
  3.3 0.1 copy-done.3
  3.4 0.0 copy-done.5
  3.4 25.3 %shard_map.86 = (bf16[4,2,8,1408]{3,2,1,0:T(8,128)(2,1)S(1)}, bf16[32,16,128]{2,1,0:T(8,128)(2,1)S(1)}) custom-call(s32[64]{0:T(128)S(1)} %copy-done.5, s32[64]{0:T(128)S(1)} %copy-done.3, bf16[64,64]{1,0:T(8,128)(2,1)S(1)} %copy-done.2, s32[640]{0:T(1024)S(1)} %copy-done.4, bf16[32,16,128]{2,1,0:T(8,128)(2,1)S(1)} %bitcast.19, bf16[8,1408]{1,0:T(8,128)(2,1)S(1)} %copy-done.1), custom_call_target="tpu_custom_call" | custom-call | tf_op jit(solution)/shard_map/pallas_call | solution.py:332
  28.7 0.7 %copy.22 = bf16[8,8,1408]{2,0,1:T(8,128)(2,1)} copy(bf16[8,8,1408]{2,1,0:T(8,128)(2,1)S(1)} %bitcast.20) | data formatting | bytes 360448 | tf_op jit(solution)/shard_map/reshape | solution.py:410
  29.4 0.2 fusion.1
  29.6 0.7 %copy.13 = bf16[2,80,4,64]{1,3,2,0:T(8,128)(2,1)} copy(bf16[2,80,4,64]{1,3,0,2:T(8,128)(2,1)S(1)} %fusion.1) | data formatting | bytes 163840
Async XLA Ops:
  0.6 0.9 %copy-start = (bf16[2,80,4,64]{1,3,2,0:T(8,128)(2,1)S(1)}, bf16[2,80,4,64]{1,3,2,0:T(8,128)(2,1)}, u32[]{:S(2)}) copy-start(bf16[2,80,4,64]{1,3,2,0:T(8,128)(2,1)} %param.7) | copy-start | bytes 245764
  2.6 0.7 %copy-start.1 = (bf16[8,1408]{1,0:T(8,128)(2,1)S(1)}, bf16[8,1408]{1,0:T(8,128)(2,1)}, u32[]{:S(2)}) copy-start(bf16[8,1408]{1,0:T(8,128)(2,1)} %factor_ref.1) | copy-start | bytes 67588
  2.6 0.7 %copy-start.2 = (bf16[64,64]{1,0:T(8,128)(2,1)S(1)}, bf16[64,64]{1,0:T(8,128)(2,1)}, u32[]{:S(2)}) copy-start(bf16[64,64]{1,0:T(8,128)(2,1)} %constant.7.clone.order_ref) | copy-start | bytes 24580
  2.6 0.7 %copy-start.4 = (s32[640]{0:T(1024)S(1)}, s32[640]{0:T(1024)}, u32[]{:S(2)}) copy-start(s32[640]{0:T(1024)} %pair_band_ref.1) | copy-start | bytes 7684
  2.8 0.7 %copy-start.3 = (s32[64]{0:T(128)S(1)}, s32[64]{0:T(128)}, u32[]{:S(2)}) copy-start(s32[64]{0:T(128)} %latitude_ref.1) | copy-start | bytes 772
  2.8 0.7 %copy-start.5 = (s32[64]{0:T(128)S(1)}, s32[64]{0:T(128)}, u32[]{:S(2)}) copy-start(s32[64]{0:T(128)} %cycle_ref.1) | copy-start | bytes 772

commit v5 on v4

--- a/solution.py
+++ b/solution.py
@@ -293,7 +293,7 @@
             finished[own, :] = jnp.concatenate(pieces, axis=1) * scale
         return carry
 
-    lax.fori_loop(0, rows, one_row, 0)
+    lax.fori_loop(0, rows, one_row, 0, unroll=True)
     pieces = []
     for member in range(2):
         columns = slice(member * half, (member + 1) * half)

time: 30.5 us -> 29.9 us (0.980)
  Pallas kernels: 25.3 us -> 24.8 us
    pallas_call x1, Pallas kernels: 25.3 us -> 24.8 us  [round_trip(): pl.pallas_call(functools.partial(round_kernel, bands, lanes), in_specs=[p...]
where the time goes in v5:
time: 29.9 us; the launch traced here: 29.7 us
  Pallas kernels  24.8 us (83%)
  local copies, waits for them, and re-layouts  3.21 us (11%)
  matrix products  1.04 us (3%)
  between operations  0.72 us (2%)
    pallas_call x1, Pallas kernels, round_trip(): pl.pallas_call(functools.partial(round_kernel, bands, lanes), in_specs=[p...  24.8 us
    unnamed x14, local copies, waits for them, and re-layouts  2.38 us
    dot_general x1, matrix products, on_device(): jnp.einsum('rl,fstl->rtfs', onehot.astype(jnp.bfloat16), coefficients, pr...  0.88 us
    reshape x1, local copies, waits for them, and re-layouts, on_device(): grid_rows = blocks.reshape(lanes * own_rows, fields, points)[:band_rows]  0.69 us

profile of v5, /device:TPU:0, one launch (start us, length us, event | category | flops | bytes accessed | tf_op | source)
XLA Modules:
  0.0 29.7 jit_solution(4722564872617865267)
XLA Ops:
  0.6 0.0 copy-start
  0.6 0.9 %copy-done = bf16[2,80,4,64]{1,3,2,0:T(8,128)(2,1)S(1)} copy-done((bf16[2,80,4,64]{1,3,2,0:T(8,128)(2,1)S(1)}, bf16[2,80,4,64]{1,3,2,0:T(8,128)(2,1)}, u32[]{:S(2)}) %copy-start) | copy-done | bytes 81944
  1.5 0.9 %fusion = bf16[64,4,2,80]{3,0,1,2:T(8,128)(2,1)S(1)} fusion(bf16[2,80,4,64]{1,3,2,0:T(8,128)(2,1)S(1)} %copy-done, s32[64]{0:T(128)} %latitude_ref.1), kind=kOutput, calls=%fused_computation.2 | convolution fusion | flops 5287936 | bytes 164096 | tf_op jit(solution)/shard_map/rl,fstl->rtfs/dot_general | solution.py:385
  2.4 0.1 copy.18
  2.6 0.0 copy-start.1
  2.6 0.0 copy-start.2
  2.6 0.0 copy-start.4
  2.6 0.1 pad.4.clone
  2.8 0.0 copy-start.3
  2.8 0.0 copy-start.5
  2.8 0.5 %copy-done.1 = bf16[8,1408]{1,0:T(8,128)(2,1)S(1)} copy-done((bf16[8,1408]{1,0:T(8,128)(2,1)S(1)}, bf16[8,1408]{1,0:T(8,128)(2,1)}, u32[]{:S(2)}) %copy-start.1) | copy-done | bytes 22552
  3.3 0.0 copy-done.2
  3.3 0.0 copy-done.4
  3.3 0.1 copy-done.3
  3.4 0.0 copy-done.5
  3.4 24.8 %shard_map.86 = (bf16[4,2,8,1408]{3,2,1,0:T(8,128)(2,1)S(1)}, bf16[32,16,128]{2,1,0:T(8,128)(2,1)S(1)}) custom-call(s32[64]{0:T(128)S(1)} %copy-done.5, s32[64]{0:T(128)S(1)} %copy-done.3, bf16[64,64]{1,0:T(8,128)(2,1)S(1)} %copy-done.2, s32[640]{0:T(1024)S(1)} %copy-done.4, bf16[32,16,128]{2,1,0:T(8,128)(2,1)S(1)} %bitcast.19, bf16[8,1408]{1,0:T(8,128)(2,1)S(1)} %copy-done.1), custom_call_target="tpu_custom_call" | custom-call | tf_op jit(solution)/shard_map/pallas_call | solution.py:332
  28.2 0.7 %copy.22 = bf16[8,8,1408]{2,0,1:T(8,128)(2,1)} copy(bf16[8,8,1408]{2,1,0:T(8,128)(2,1)S(1)} %bitcast.20) | data formatting | bytes 360448 | tf_op jit(solution)/shard_map/reshape | solution.py:410
  28.9 0.2 fusion.1
  29.1 0.7 %copy.13 = bf16[2,80,4,64]{1,3,2,0:T(8,128)(2,1)} copy(bf16[2,80,4,64]{1,3,0,2:T(8,128)(2,1)S(1)} %fusion.1) | data formatting | bytes 163840
Async XLA Ops:
  0.6 0.9 %copy-start = (bf16[2,80,4,64]{1,3,2,0:T(8,128)(2,1)S(1)}, bf16[2,80,4,64]{1,3,2,0:T(8,128)(2,1)}, u32[]{:S(2)}) copy-start(bf16[2,80,4,64]{1,3,2,0:T(8,128)(2,1)} %param.7) | copy-start | bytes 245764
  2.6 0.7 %copy-start.1 = (bf16[8,1408]{1,0:T(8,128)(2,1)S(1)}, bf16[8,1408]{1,0:T(8,128)(2,1)}, u32[]{:S(2)}) copy-start(bf16[8,1408]{1,0:T(8,128)(2,1)} %factor_ref.1) | copy-start | bytes 67588
  2.6 0.7 %copy-start.2 = (bf16[64,64]{1,0:T(8,128)(2,1)S(1)}, bf16[64,64]{1,0:T(8,128)(2,1)}, u32[]{:S(2)}) copy-start(bf16[64,64]{1,0:T(8,128)(2,1)} %constant.7.clone.order_ref) | copy-start | bytes 24580
  2.6 0.7 %copy-start.4 = (s32[640]{0:T(1024)S(1)}, s32[640]{0:T(1024)}, u32[]{:S(2)}) copy-start(s32[640]{0:T(1024)} %pair_band_ref.1) | copy-start | bytes 7684
  2.8 0.7 %copy-start.3 = (s32[64]{0:T(128)S(1)}, s32[64]{0:T(128)}, u32[]{:S(2)}) copy-start(s32[64]{0:T(128)} %latitude_ref.1) | copy-start | bytes 772
  2.8 0.7 %copy-start.5 = (s32[64]{0:T(128)S(1)}, s32[64]{0:T(128)}, u32[]{:S(2)}) copy-start(s32[64]{0:T(128)} %cycle_ref.1) | copy-start | bytes 772
